TPU v7x, 32 devices: a whole 2x2x4 slice. The times are simulated.
32 devices in a mesh: case: 2 (over y), blk: 4 (over z), freq: 4 (over x, core).
Axes of the slice: x: 2, y: 2, z: 4, core: 2. Of those that a mesh axis runs over, the one named last changes fastest.
Arguments:
- geometry: bfloat16 [3, 8192], P(None, ('case', 'blk')), parts along dimension 1, may hold values from -4 to 4
- modes: bfloat16 [4, 8192, 128], P('freq', ('case', 'blk')), parts along dimension 1, may hold values from -6 to 6
- reduced_freq: float32 [16], replicated, may hold values from 0.1 to 1.5
- freq_index: int32 [8, 3], P(('case', 'freq')), parts along dimension 0, may hold values from 0 to 15
Outputs:
- grad_geometry: float32 [3, 8192], P(None, ('case', 'blk', 'freq')), parts along dimension 1
- forces: float32 [8, 2, 32, 32], P(('case', 'freq')), parts along dimension 0
There are 2 independent parts, one for each index of `case`. A program takes and returns all parts, laid end to end along the dimension named above; an argument that names none is the same for every part. Nothing has to cross between parts.
All inputs are finite; a program needn't handle non-finite values.
Results may differ from a plain program's by a relative error of at most 0.003.
Values may be sent and summed in bfloat16 or wider, within the bound.
No kernel may reach another device: no remote copies, remote signals or barrier semaphores. Data moves between devices by JAX's collectives and lax.ppermute only.
A program may use at most 64 MiB of HBM per device.

v0:
```python
import math

import jax
import jax.numpy as jnp
from jax import lax
from jax.sharding import PartitionSpec as P

CHORD_SHIFT = 0.5
CORE_SQUARE = 0.25


def passed_along(value, axis, steps):
    count = lax.axis_size(axis)
    pairs = [(source, (source + steps) % count) for source in range(count)]
    return lax.ppermute(value, axis, pairs)


def prepare_sender(send_modes):
    columns = send_modes.shape[1] // 4
    flipped = jnp.concatenate([send_modes[:, 2 * columns :], send_modes[:, : 2 * columns]], axis=1)
    turned = jnp.concatenate(
        [
            send_modes[:, 3 * columns :],
            -send_modes[:, 2 * columns : 3 * columns],
            send_modes[:, columns : 2 * columns],
            -send_modes[:, :columns],
        ],
        axis=1,
    )
    paired = jnp.concatenate([flipped, turned], axis=0)
    strength = jnp.concatenate(
        [
            send_modes[:, 2 * columns :],
            jnp.concatenate(
                [-send_modes[:, 3 * columns :], send_modes[:, 2 * columns : 3 * columns]], axis=1
            ),
        ],
        axis=0,
    )
    return (paired, strength)


def block_terms(recv_geom, recv_modes, send_pos, paired, strength, wavenumber):
    send_count = send_pos.shape[1]
    coupled = lax.dot_general(
        recv_modes, paired, (((1,), (1,)), ((), ())), preferred_element_type=jnp.float32
    )
    real_part = coupled[:, :send_count]
    imag_part = coupled[:, send_count:]
    recv_pos = recv_geom.astype(jnp.float32)
    delta_x = recv_pos[0][:, None] + CHORD_SHIFT - send_pos[0][None, :]
    delta_y = recv_pos[1][:, None] - send_pos[1][None, :]
    delta_z = recv_pos[2][:, None] - send_pos[2][None, :]
    inverse = lax.rsqrt(delta_x * delta_x + delta_y * delta_y + delta_z * delta_z + CORE_SQUARE)
    phase = wavenumber * delta_x
    cosine = jnp.cos(phase)
    sine = jnp.sin(phase)
    along = cosine * real_part + sine * imag_part
    across = cosine * imag_part - sine * real_part
    cubed = inverse * inverse * inverse * along
    grad_x = wavenumber * inverse * across - delta_x * cubed
    grad_y = -delta_y * cubed
    grad_z = -delta_z * cubed
    row_grad = jnp.stack([grad_x.sum(axis=1), grad_y.sum(axis=1), grad_z.sum(axis=1)])
    col_grad = -jnp.stack([grad_x.sum(axis=0), grad_y.sum(axis=0), grad_z.sum(axis=0)])
    kernel = jnp.concatenate([cosine * inverse, -sine * inverse], axis=1).astype(jnp.bfloat16)
    pressure = jnp.dot(kernel, strength, preferred_element_type=jnp.float32)
    return (row_grad, col_grad, pressure)


def spread(stacked):
    return lax.psum_scatter(stacked, "freq", scatter_dimension=2, tiled=True)


def local(geometry, modes, reduced_freq, freq_index):
    row_count = geometry.shape[1]
    own_modes = modes[0]
    columns = own_modes.shape[1] // 4
    steps = freq_index.shape[1]
    table_size = reduced_freq.shape[0]
    selected = freq_index[0][:, None] == jnp.arange(table_size, dtype=jnp.int32)[None, :]
    wavenumbers = jnp.sum(jnp.where(selected, reduced_freq[None, :], 0.0), axis=1)
    local_block = (geometry, own_modes)
    sending = [local_block]
    current = local_block
    for offset in range(1, steps):
        current = passed_along((current[0], current[1]), "blk", 1)
        sending.append(current)
    block_rows = min(128, row_count)
    block_count = row_count // block_rows
    recv_geom = geometry.reshape(3, block_count, block_rows).transpose(1, 0, 2)
    recv_modes = own_modes.reshape(block_count, block_rows, 4 * columns)
    row_total = jnp.zeros((3, row_count), jnp.float32)
    pressure_total = jnp.zeros((row_count, 2 * columns), jnp.float32)
    col_parts = []
    for offset in range(steps):
        send_geom, send_modes = sending[offset]
        paired, strength = prepare_sender(send_modes)
        send_pos = send_geom.astype(jnp.float32)
        wavenumber = wavenumbers[offset]

        def visit(
            carry,
            operands,
            send_pos=send_pos,
            paired=paired,
            strength=strength,
            wavenumber=wavenumber,
        ):
            row_grad, col_grad, pressure = block_terms(
                operands[0], operands[1], send_pos, paired, strength, wavenumber
            )
            return (carry + col_grad, (row_grad, pressure))

        col_grad, (row_parts, pressure_parts) = lax.scan(
            visit, jnp.zeros((3, row_count), jnp.float32), (recv_geom, recv_modes)
        )
        row_total = row_total + row_parts.transpose(1, 0, 2).reshape(3, row_count)
        pressure_total = pressure_total + pressure_parts.reshape(row_count, 2 * columns)
        col_parts.append(col_grad)
    local_grad = row_total + col_parts[0]
    grad_scale = 1.0 / math.sqrt(columns * steps * row_count * lax.axis_size("freq"))
    total = local_grad
    for offset in range(1, steps):
        total = total + passed_along(col_parts[offset], "blk", -offset)
    result = spread((total * grad_scale)[None])[0]
    adjoint = own_modes[:, : 2 * columns].astype(jnp.float32)
    adj_real = adjoint[:, :columns]
    adj_imag = adjoint[:, columns:]
    press_real = pressure_total[:, :columns]
    press_imag = pressure_total[:, columns:]
    contract = (((0,), (0,)), ((), ()))
    force_real = lax.dot_general(
        adj_real, press_real, contract, precision=lax.Precision.HIGHEST
    ) + lax.dot_general(adj_imag, press_imag, contract, precision=lax.Precision.HIGHEST)
    force_imag = lax.dot_general(
        adj_real, press_imag, contract, precision=lax.Precision.HIGHEST
    ) - lax.dot_general(adj_imag, press_real, contract, precision=lax.Precision.HIGHEST)
    force_local = jnp.stack([force_real, force_imag])
    force_total = lax.psum(force_local, "blk")
    force_scale = 1.0 / math.sqrt(row_count * row_count * lax.axis_size("blk") * steps)
    return (result, (force_total * force_scale)[None])


def solution(mesh):
    return jax.shard_map(
        local,
        mesh=mesh,
        in_specs=(
            P(None, ("case", "blk")),
            P("freq", ("case", "blk"), None),
            P(),
            P(("case", "freq"), None),
        ),
        out_specs=(P(None, ("case", "blk", "freq")), P(("case", "freq"), None, None, None)),
        check_vma=False,
    )
```

profile of v0, /device:TPU:0, one launch (start us, length us, event | category | flops | bytes accessed | tf_op | source)
XLA Modules:
  0.0 178.1 jit_solution(9225079058068563746)
XLA Ops:
  7.2 3.1 %collective-permute-start.1 = (bf16[1024,128]{1,0:T(8,128)(2,1)}, bf16[1024,128]{1,0:T(8,128)(2,1)S(1)}, u32[]{:S(2)}, u32[]{:S(2)}) collective-permute-start(bf16[1024,128]{1,0:T(8,128)(2,1)} %bitcast.219), channel_id=1, source_target_pairs={{0,4},{4,8},{8,12},{12,0},{1,5},{5,9},{9,13},{13,1},{2,6},{6,10},{... | collective-permute-start | bytes 786440 | tf_op jit(solution)/shard_map/ppermute | solution.py:15
  10.3 1.6 collective-permute-start
  11.9 1.7 slice_negate_fusion.8
  13.7 0.6 copy-done.2
  14.8 0.5 maximum_maximum_fusion
  15.3 0.7 fusion.139
  16.0 3.0 %collective-permute-done = bf16[3,1024]{1,0:T(4,128)(2,1)S(1)} collective-permute-done((bf16[3,1024]{1,0:T(4,128)(2,1)}, bf16[3,1024]{1,0:T(4,128)(2,1)S(1)}, u32[]{:S(2)}, u32[]{:S(2)}) %collective-permute-start) | collective-permute-done | bytes 6176 | tf_op jit(solution)/shard_map/ppermute | solution.py:15
  19.0 34.4 %while.45 = (s32[]{:T(128)}, f32[3,1024]{1,0:T(4,128)S(1)}, f32[8,3,128]{2,1,0:T(4,128)S(1)}, f32[8,128,64]{1,2,0:T(8,128)S(1)}, f32[]{:T(128)}, /*index=5*/bf16...) while((s32[]{:T(128)}, f32[3,1024]{1,0:T(4,128)S(1)}, ...), condition=%wide.region_8.9_spmd.clone, body=%wide.region_1.8_spmd.clone.sunk | while | flops 106967936 | bytes 6464403 | solution.py:115
  19.4 3.2 %fusion.185 = (bf16[128,1024]{1,0:T(8,128)(2,1)S(1)}, bf16[128,1024]{1,0:T(8,128)(2,1)S(1)}, f32[128,1024]{1,0:T(8,128)S(1)}, f32[128,1024]{1,0:T(8,128)S(1)}) fusion(f32[1024]{0:T(1024)S(1)} %bitcast.228, f32[128]{0:T(128)S(1)} %get-tuple-element.645, f32[1024]{0:T(1024)S(1)} %bitcast.230, f32[128]{0:T(128)S(1)} %get-tuple-element.647, ...), kind=kLoop, calls=%fused_computation.25.clone.1 | loop fusion | flops 3670016 | bytes 2635268 | tf_op jit(solution)/shard_map/convert
  23.7 3.2 %fusion.185 = (bf16[128,1024]{1,0:T(8,128)(2,1)S(1)}, bf16[128,1024]{1,0:T(8,128)(2,1)S(1)}, f32[128,1024]{1,0:T(8,128)S(1)}, f32[128,1024]{1,0:T(8,128)S(1)}) fusion(f32[1024]{0:T(1024)S(1)} %bitcast.228, f32[128]{0:T(128)S(1)} %get-tuple-element.645, f32[1024]{0:T(1024)S(1)} %bitcast.230, f32[128]{0:T(128)S(1)} %get-tuple-element.647, ...), kind=kLoop, calls=%fused_computation.25.clone.1 | loop fusion | flops 3670016 | bytes 2635268 | tf_op jit(solution)/shard_map/convert
  27.2 0.4 fusion.186
  28.0 3.2 %fusion.185 = (bf16[128,1024]{1,0:T(8,128)(2,1)S(1)}, bf16[128,1024]{1,0:T(8,128)(2,1)S(1)}, f32[128,1024]{1,0:T(8,128)S(1)}, f32[128,1024]{1,0:T(8,128)S(1)}) fusion(f32[1024]{0:T(1024)S(1)} %bitcast.228, f32[128]{0:T(128)S(1)} %get-tuple-element.645, f32[1024]{0:T(1024)S(1)} %bitcast.230, f32[128]{0:T(128)S(1)} %get-tuple-element.647, ...), kind=kLoop, calls=%fused_computation.25.clone.1 | loop fusion | flops 3670016 | bytes 2635268 | tf_op jit(solution)/shard_map/convert
  32.3 3.2 %fusion.185 = (bf16[128,1024]{1,0:T(8,128)(2,1)S(1)}, bf16[128,1024]{1,0:T(8,128)(2,1)S(1)}, f32[128,1024]{1,0:T(8,128)S(1)}, f32[128,1024]{1,0:T(8,128)S(1)}) fusion(f32[1024]{0:T(1024)S(1)} %bitcast.228, f32[128]{0:T(128)S(1)} %get-tuple-element.645, f32[1024]{0:T(1024)S(1)} %bitcast.230, f32[128]{0:T(128)S(1)} %get-tuple-element.647, ...), kind=kLoop, calls=%fused_computation.25.clone.1 | loop fusion | flops 3670016 | bytes 2635268 | tf_op jit(solution)/shard_map/convert
  36.6 3.2 %fusion.185 = (bf16[128,1024]{1,0:T(8,128)(2,1)S(1)}, bf16[128,1024]{1,0:T(8,128)(2,1)S(1)}, f32[128,1024]{1,0:T(8,128)S(1)}, f32[128,1024]{1,0:T(8,128)S(1)}) fusion(f32[1024]{0:T(1024)S(1)} %bitcast.228, f32[128]{0:T(128)S(1)} %get-tuple-element.645, f32[1024]{0:T(1024)S(1)} %bitcast.230, f32[128]{0:T(128)S(1)} %get-tuple-element.647, ...), kind=kLoop, calls=%fused_computation.25.clone.1 | loop fusion | flops 3670016 | bytes 2635268 | tf_op jit(solution)/shard_map/convert
  40.9 3.2 %fusion.185 = (bf16[128,1024]{1,0:T(8,128)(2,1)S(1)}, bf16[128,1024]{1,0:T(8,128)(2,1)S(1)}, f32[128,1024]{1,0:T(8,128)S(1)}, f32[128,1024]{1,0:T(8,128)S(1)}) fusion(f32[1024]{0:T(1024)S(1)} %bitcast.228, f32[128]{0:T(128)S(1)} %get-tuple-element.645, f32[1024]{0:T(1024)S(1)} %bitcast.230, f32[128]{0:T(128)S(1)} %get-tuple-element.647, ...), kind=kLoop, calls=%fused_computation.25.clone.1 | loop fusion | flops 3670016 | bytes 2635268 | tf_op jit(solution)/shard_map/convert
  44.4 0.4 fusion.186
  45.2 3.2 %fusion.185 = (bf16[128,1024]{1,0:T(8,128)(2,1)S(1)}, bf16[128,1024]{1,0:T(8,128)(2,1)S(1)}, f32[128,1024]{1,0:T(8,128)S(1)}, f32[128,1024]{1,0:T(8,128)S(1)}) fusion(f32[1024]{0:T(1024)S(1)} %bitcast.228, f32[128]{0:T(128)S(1)} %get-tuple-element.645, f32[1024]{0:T(1024)S(1)} %bitcast.230, f32[128]{0:T(128)S(1)} %get-tuple-element.647, ...), kind=kLoop, calls=%fused_computation.25.clone.1 | loop fusion | flops 3670016 | bytes 2635268 | tf_op jit(solution)/shard_map/convert
  49.5 3.2 %fusion.185 = (bf16[128,1024]{1,0:T(8,128)(2,1)S(1)}, bf16[128,1024]{1,0:T(8,128)(2,1)S(1)}, f32[128,1024]{1,0:T(8,128)S(1)}, f32[128,1024]{1,0:T(8,128)S(1)}) fusion(f32[1024]{0:T(1024)S(1)} %bitcast.228, f32[128]{0:T(128)S(1)} %get-tuple-element.645, f32[1024]{0:T(1024)S(1)} %bitcast.230, f32[128]{0:T(128)S(1)} %get-tuple-element.647, ...), kind=kLoop, calls=%fused_computation.25.clone.1 | loop fusion | flops 3670016 | bytes 2635268 | tf_op jit(solution)/shard_map/convert
  53.0 0.4 fusion.186
  54.2 0.5 maximum_maximum_fusion.2
  54.7 1.3 collective-permute-start.3
  56.0 34.7 %while.46 = (s32[]{:T(128)}, f32[3,1024]{1,0:T(4,128)S(1)}, f32[8,3,128]{2,1,0:T(4,128)S(1)}, f32[8,128,64]{1,2,0:T(8,128)S(1)}, f32[]{:T(128)}, /*index=5*/bf16...) while((s32[]{:T(128)}, f32[3,1024]{1,0:T(4,128)S(1)}, ...), condition=%wide.region_16.17_spmd.clone, body=%wide.region_9.16_spmd.clone.sunk | while | flops 106967936 | bytes 6464403 | solution.py:115
  56.4 3.2 %fusion.196 = (bf16[128,1024]{1,0:T(8,128)(2,1)S(1)}, bf16[128,1024]{1,0:T(8,128)(2,1)S(1)}, f32[128,1024]{1,0:T(8,128)S(1)}, f32[128,1024]{1,0:T(8,128)S(1)}) fusion(f32[1024]{0:T(1024)S(1)} %bitcast.232, f32[128]{0:T(128)S(1)} %get-tuple-element.671, f32[1024]{0:T(1024)S(1)} %bitcast.234, f32[128]{0:T(128)S(1)} %get-tuple-element.673, ...), kind=kLoop, calls=%fused_computation.77.clone.1 | loop fusion | flops 3670016 | bytes 2635268 | tf_op jit(solution)/shard_map/convert.2
  60.8 3.2 %fusion.196 = (bf16[128,1024]{1,0:T(8,128)(2,1)S(1)}, bf16[128,1024]{1,0:T(8,128)(2,1)S(1)}, f32[128,1024]{1,0:T(8,128)S(1)}, f32[128,1024]{1,0:T(8,128)S(1)}) fusion(f32[1024]{0:T(1024)S(1)} %bitcast.232, f32[128]{0:T(128)S(1)} %get-tuple-element.671, f32[1024]{0:T(1024)S(1)} %bitcast.234, f32[128]{0:T(128)S(1)} %get-tuple-element.673, ...), kind=kLoop, calls=%fused_computation.77.clone.1 | loop fusion | flops 3670016 | bytes 2635268 | tf_op jit(solution)/shard_map/convert.2
  65.1 3.2 %fusion.196 = (bf16[128,1024]{1,0:T(8,128)(2,1)S(1)}, bf16[128,1024]{1,0:T(8,128)(2,1)S(1)}, f32[128,1024]{1,0:T(8,128)S(1)}, f32[128,1024]{1,0:T(8,128)S(1)}) fusion(f32[1024]{0:T(1024)S(1)} %bitcast.232, f32[128]{0:T(128)S(1)} %get-tuple-element.671, f32[1024]{0:T(1024)S(1)} %bitcast.234, f32[128]{0:T(128)S(1)} %get-tuple-element.673, ...), kind=kLoop, calls=%fused_computation.77.clone.1 | loop fusion | flops 3670016 | bytes 2635268 | tf_op jit(solution)/shard_map/convert.2
  69.4 3.2 %fusion.196 = (bf16[128,1024]{1,0:T(8,128)(2,1)S(1)}, bf16[128,1024]{1,0:T(8,128)(2,1)S(1)}, f32[128,1024]{1,0:T(8,128)S(1)}, f32[128,1024]{1,0:T(8,128)S(1)}) fusion(f32[1024]{0:T(1024)S(1)} %bitcast.232, f32[128]{0:T(128)S(1)} %get-tuple-element.671, f32[1024]{0:T(1024)S(1)} %bitcast.234, f32[128]{0:T(128)S(1)} %get-tuple-element.673, ...), kind=kLoop, calls=%fused_computation.77.clone.1 | loop fusion | flops 3670016 | bytes 2635268 | tf_op jit(solution)/shard_map/convert.2
  73.8 3.2 %fusion.196 = (bf16[128,1024]{1,0:T(8,128)(2,1)S(1)}, bf16[128,1024]{1,0:T(8,128)(2,1)S(1)}, f32[128,1024]{1,0:T(8,128)S(1)}, f32[128,1024]{1,0:T(8,128)S(1)}) fusion(f32[1024]{0:T(1024)S(1)} %bitcast.232, f32[128]{0:T(128)S(1)} %get-tuple-element.671, f32[1024]{0:T(1024)S(1)} %bitcast.234, f32[128]{0:T(128)S(1)} %get-tuple-element.673, ...), kind=kLoop, calls=%fused_computation.77.clone.1 | loop fusion | flops 3670016 | bytes 2635268 | tf_op jit(solution)/shard_map/convert.2
  78.1 3.2 %fusion.196 = (bf16[128,1024]{1,0:T(8,128)(2,1)S(1)}, bf16[128,1024]{1,0:T(8,128)(2,1)S(1)}, f32[128,1024]{1,0:T(8,128)S(1)}, f32[128,1024]{1,0:T(8,128)S(1)}) fusion(f32[1024]{0:T(1024)S(1)} %bitcast.232, f32[128]{0:T(128)S(1)} %get-tuple-element.671, f32[1024]{0:T(1024)S(1)} %bitcast.234, f32[128]{0:T(128)S(1)} %get-tuple-element.673, ...), kind=kLoop, calls=%fused_computation.77.clone.1 | loop fusion | flops 3670016 | bytes 2635268 | tf_op jit(solution)/shard_map/convert.2
  82.5 3.2 %fusion.196 = (bf16[128,1024]{1,0:T(8,128)(2,1)S(1)}, bf16[128,1024]{1,0:T(8,128)(2,1)S(1)}, f32[128,1024]{1,0:T(8,128)S(1)}, f32[128,1024]{1,0:T(8,128)S(1)}) fusion(f32[1024]{0:T(1024)S(1)} %bitcast.232, f32[128]{0:T(128)S(1)} %get-tuple-element.671, f32[1024]{0:T(1024)S(1)} %bitcast.234, f32[128]{0:T(128)S(1)} %get-tuple-element.673, ...), kind=kLoop, calls=%fused_computation.77.clone.1 | loop fusion | flops 3670016 | bytes 2635268 | tf_op jit(solution)/shard_map/convert.2
  86.8 3.2 %fusion.196 = (bf16[128,1024]{1,0:T(8,128)(2,1)S(1)}, bf16[128,1024]{1,0:T(8,128)(2,1)S(1)}, f32[128,1024]{1,0:T(8,128)S(1)}, f32[128,1024]{1,0:T(8,128)S(1)}) fusion(f32[1024]{0:T(1024)S(1)} %bitcast.232, f32[128]{0:T(128)S(1)} %get-tuple-element.671, f32[1024]{0:T(1024)S(1)} %bitcast.234, f32[128]{0:T(128)S(1)} %get-tuple-element.673, ...), kind=kLoop, calls=%fused_computation.77.clone.1 | loop fusion | flops 3670016 | bytes 2635268 | tf_op jit(solution)/shard_map/convert.2
  90.8 2.6 %collective-permute-start.4 = (f32[3,1024]{1,0:T(4,128)S(1)}, f32[3,1024]{1,0:T(4,128)S(1)}, u32[]{:S(2)}, u32[]{:S(2)}) collective-permute-start(f32[3,1024]{1,0:T(4,128)S(1)} %get-tuple-element.168), channel_id=1, source_target_pairs={{0,12},{4,0},{8,4},{12,8},{1,13},{5,1},{9,5},{13,9},{2,14},{6,2},{... | collective-permute-start | bytes 36872 | tf_op jit(solution)/shard_map/ppermute | solution.py:15
  94.0 0.5 maximum_maximum_fusion.4
  94.6 34.4 %while.47 = (s32[]{:T(128)}, f32[3,1024]{1,0:T(4,128)S(1)}, f32[8,3,128]{2,1,0:T(4,128)S(1)}, f32[8,128,64]{1,2,0:T(8,128)S(1)}, f32[]{:T(128)}, /*index=5*/bf16...) while((s32[]{:T(128)}, f32[3,1024]{1,0:T(4,128)S(1)}, ...), condition=%wide.region_24.25_spmd.clone, body=%wide.region_17.24_spmd.clone.sunk | while | flops 106967936 | bytes 6464403 | solution.py:115
  94.9 3.2 %fusion.207 = (bf16[128,1024]{1,0:T(8,128)(2,1)S(1)}, bf16[128,1024]{1,0:T(8,128)(2,1)S(1)}, f32[128,1024]{1,0:T(8,128)S(1)}, f32[128,1024]{1,0:T(8,128)S(1)}) fusion(f32[1024]{0:T(1024)S(1)} %bitcast.236, f32[128]{0:T(128)S(1)} %get-tuple-element.697, f32[1024]{0:T(1024)S(1)} %bitcast.238, f32[128]{0:T(128)S(1)} %get-tuple-element.699, ...), kind=kLoop, calls=%fused_computation.129.clone.1 | loop fusion | flops 3670016 | bytes 2635268 | tf_op jit(solution)/shard_map/convert.4
  99.2 3.2 %fusion.207 = (bf16[128,1024]{1,0:T(8,128)(2,1)S(1)}, bf16[128,1024]{1,0:T(8,128)(2,1)S(1)}, f32[128,1024]{1,0:T(8,128)S(1)}, f32[128,1024]{1,0:T(8,128)S(1)}) fusion(f32[1024]{0:T(1024)S(1)} %bitcast.236, f32[128]{0:T(128)S(1)} %get-tuple-element.697, f32[1024]{0:T(1024)S(1)} %bitcast.238, f32[128]{0:T(128)S(1)} %get-tuple-element.699, ...), kind=kLoop, calls=%fused_computation.129.clone.1 | loop fusion | flops 3670016 | bytes 2635268 | tf_op jit(solution)/shard_map/convert.4
  103.5 3.2 %fusion.207 = (bf16[128,1024]{1,0:T(8,128)(2,1)S(1)}, bf16[128,1024]{1,0:T(8,128)(2,1)S(1)}, f32[128,1024]{1,0:T(8,128)S(1)}, f32[128,1024]{1,0:T(8,128)S(1)}) fusion(f32[1024]{0:T(1024)S(1)} %bitcast.236, f32[128]{0:T(128)S(1)} %get-tuple-element.697, f32[1024]{0:T(1024)S(1)} %bitcast.238, f32[128]{0:T(128)S(1)} %get-tuple-element.699, ...), kind=kLoop, calls=%fused_computation.129.clone.1 | loop fusion | flops 3670016 | bytes 2635268 | tf_op jit(solution)/shard_map/convert.4
  107.8 3.2 %fusion.207 = (bf16[128,1024]{1,0:T(8,128)(2,1)S(1)}, bf16[128,1024]{1,0:T(8,128)(2,1)S(1)}, f32[128,1024]{1,0:T(8,128)S(1)}, f32[128,1024]{1,0:T(8,128)S(1)}) fusion(f32[1024]{0:T(1024)S(1)} %bitcast.236, f32[128]{0:T(128)S(1)} %get-tuple-element.697, f32[1024]{0:T(1024)S(1)} %bitcast.238, f32[128]{0:T(128)S(1)} %get-tuple-element.699, ...), kind=kLoop, calls=%fused_computation.129.clone.1 | loop fusion | flops 3670016 | bytes 2635268 | tf_op jit(solution)/shard_map/convert.4
  112.2 3.2 %fusion.207 = (bf16[128,1024]{1,0:T(8,128)(2,1)S(1)}, bf16[128,1024]{1,0:T(8,128)(2,1)S(1)}, f32[128,1024]{1,0:T(8,128)S(1)}, f32[128,1024]{1,0:T(8,128)S(1)}) fusion(f32[1024]{0:T(1024)S(1)} %bitcast.236, f32[128]{0:T(128)S(1)} %get-tuple-element.697, f32[1024]{0:T(1024)S(1)} %bitcast.238, f32[128]{0:T(128)S(1)} %get-tuple-element.699, ...), kind=kLoop, calls=%fused_computation.129.clone.1 | loop fusion | flops 3670016 | bytes 2635268 | tf_op jit(solution)/shard_map/convert.4
  116.5 3.2 %fusion.207 = (bf16[128,1024]{1,0:T(8,128)(2,1)S(1)}, bf16[128,1024]{1,0:T(8,128)(2,1)S(1)}, f32[128,1024]{1,0:T(8,128)S(1)}, f32[128,1024]{1,0:T(8,128)S(1)}) fusion(f32[1024]{0:T(1024)S(1)} %bitcast.236, f32[128]{0:T(128)S(1)} %get-tuple-element.697, f32[1024]{0:T(1024)S(1)} %bitcast.238, f32[128]{0:T(128)S(1)} %get-tuple-element.699, ...), kind=kLoop, calls=%fused_computation.129.clone.1 | loop fusion | flops 3670016 | bytes 2635268 | tf_op jit(solution)/shard_map/convert.4
  120.8 3.2 %fusion.207 = (bf16[128,1024]{1,0:T(8,128)(2,1)S(1)}, bf16[128,1024]{1,0:T(8,128)(2,1)S(1)}, f32[128,1024]{1,0:T(8,128)S(1)}, f32[128,1024]{1,0:T(8,128)S(1)}) fusion(f32[1024]{0:T(1024)S(1)} %bitcast.236, f32[128]{0:T(128)S(1)} %get-tuple-element.697, f32[1024]{0:T(1024)S(1)} %bitcast.238, f32[128]{0:T(128)S(1)} %get-tuple-element.699, ...), kind=kLoop, calls=%fused_computation.129.clone.1 | loop fusion | flops 3670016 | bytes 2635268 | tf_op jit(solution)/shard_map/convert.4
  125.1 3.2 %fusion.207 = (bf16[128,1024]{1,0:T(8,128)(2,1)S(1)}, bf16[128,1024]{1,0:T(8,128)(2,1)S(1)}, f32[128,1024]{1,0:T(8,128)S(1)}, f32[128,1024]{1,0:T(8,128)S(1)}) fusion(f32[1024]{0:T(1024)S(1)} %bitcast.236, f32[128]{0:T(128)S(1)} %get-tuple-element.697, f32[1024]{0:T(1024)S(1)} %bitcast.238, f32[128]{0:T(128)S(1)} %get-tuple-element.699, ...), kind=kLoop, calls=%fused_computation.129.clone.1 | loop fusion | flops 3670016 | bytes 2635268 | tf_op jit(solution)/shard_map/convert.4
  128.6 0.4 fusion.208
  130.2 0.6 collective-permute-start.5
  130.8 17.7 %psum.7 = f32[2,32,32]{1,2,0:T(8,128)S(1)} all-reduce(f32[2,32,32]{1,2,0:T(8,128)S(1)} %pad_maximum_fusion), channel_id=1, replica_groups=mesh['case'=2,'blk'=4,'freq'=4] {'blk'}, use_global_device_ids=true, to_apply=%region_26.27 | all-reduce | flops 2048 | bytes 16384 | tf_op jit(solution)/shard_map/psum | solution.py:140
  148.6 1.0 copy.13
  149.7 0.7 copy.12
  150.4 19.2 %reduce-scatter.4.cloned.1.call-done = f32[256,3]{1,0:T(8,128)} async-done(((f32[1024,3]{1,0:T(8,128)}), f32[256,3]{1,0:T(8,128)}) %reduce-scatter.4.cloned.1.call-update) | async-done | bytes 3088
  169.6 1.6 copy.14
  (232 shorter events, 27.6 us)
Async XLA Ops:
  7.2 162.5 %reduce-scatter.4.cloned.1.call-start = ((), (), s32[]{:S(2)}) async-start(), calls=%async_computation.1 | async-start | bytes 655360
  7.2 46.3 %collective-permute-start.1 = (bf16[1024,128]{1,0:T(8,128)(2,1)}, bf16[1024,128]{1,0:T(8,128)(2,1)S(1)}, u32[]{:S(2)}, u32[]{:S(2)}) collective-permute-start(bf16[1024,128]{1,0:T(8,128)(2,1)} %bitcast.219), channel_id=1, source_target_pairs={{0,4},{4,8},{8,12},{12,0},{1,5},{5,9},{9,13},{13,1},{2,6},{6,10},{... | collective-permute-start | bytes 786440 | tf_op jit(solution)/shard_map/ppermute | solution.py:15
  10.3 8.7 %collective-permute-start = (bf16[3,1024]{1,0:T(4,128)(2,1)}, bf16[3,1024]{1,0:T(4,128)(2,1)S(1)}, u32[]{:S(2)}, u32[]{:S(2)}) collective-permute-start(bf16[3,1024]{1,0:T(4,128)(2,1)} %param.10), channel_id=1, source_target_pairs={{0,4},{4,8},{8,12},{12,0},{1,5},{5,9},{9,13},{13,1},{2,6},{6,10},{... | collective-permute-start | bytes 18440 | tf_op jit(solution)/shard_map/ppermute | solution.py:15
  11.9 1.7 copy-start
  13.7 0.7 copy-start.2
  13.7 0.7 copy-start.3
  14.8 1.2 copy-start.1
  19.0 34.5 %collective-permute-start.2 = (bf16[3,1024]{1,0:T(4,128)(2,1)S(1)}, bf16[3,1024]{1,0:T(4,128)(2,1)S(1)}, u32[]{:S(2)}, u32[]{:S(2)}) collective-permute-start(bf16[3,1024]{1,0:T(4,128)(2,1)S(1)} %collective-permute-done), channel_id=1, source_target_pairs={{0,4},{4,8},{8,12},{12,0},{1,5},{5,9},{9,13},{13,1},{2,6},{6,10},{... | collective-permute-start | bytes 18440 | tf_op jit(solution)/shard_map/ppermute | solution.py:15
  54.7 38.7 %collective-permute-start.3 = (bf16[1024,128]{1,0:T(8,128)(2,1)S(1)}, bf16[1024,128]{1,0:T(8,128)(2,1)S(1)}, u32[]{:S(2)}, u32[]{:S(2)}) collective-permute-start(bf16[1024,128]{1,0:T(8,128)(2,1)S(1)} %collective-permute-done.1), channel_id=1, source_target_pairs={{0,4},{4,8},{8,12},{12,0},{1,5},{5,9},{9,13},{13,1},{2,6},{6,10},{... | collective-permute-start | bytes 786440 | tf_op jit(solution)/shard_map/ppermute | solution.py:15
  90.8 57.8 %collective-permute-start.4 = (f32[3,1024]{1,0:T(4,128)S(1)}, f32[3,1024]{1,0:T(4,128)S(1)}, u32[]{:S(2)}, u32[]{:S(2)}) collective-permute-start(f32[3,1024]{1,0:T(4,128)S(1)} %get-tuple-element.168), channel_id=1, source_target_pairs={{0,12},{4,0},{8,4},{12,8},{1,13},{5,1},{9,5},{13,9},{2,14},{6,2},{... | collective-permute-start | bytes 36872 | tf_op jit(solution)/shard_map/ppermute | solution.py:15
  130.2 18.4 %collective-permute-start.5 = (f32[3,1024]{1,0:T(4,128)S(1)}, f32[3,1024]{1,0:T(4,128)S(1)}, u32[]{:S(2)}, u32[]{:S(2)}) collective-permute-start(f32[3,1024]{1,0:T(4,128)S(1)} %get-tuple-element.169), channel_id=1, source_target_pairs={{0,8},{4,12},{8,0},{12,4},{1,9},{5,13},{9,1},{13,5},{2,10},{6,14},... | collective-permute-start | bytes 36872 | tf_op jit(solution)/shard_map/ppermute | solution.py:15
Sparse Core Ops, SparseCore 0:
  149.8 19.7 reduce-scatter.3
where the time goes:
time: 178 us
  other arithmetic  91.4 us (51%)
  waiting for transfers between devices  22.3 us (13%)
  blocking collectives  17.7 us (10%)
  matrix products  16.2 us (9%)
  between operations  14.3 us (8%)
  starting transfers between devices  9.26 us (5%)
  local copies, waits for them, and re-layouts  5.38 us (3%)
    another operation x24, other arithmetic  76.2 us
    unnamed x2, waiting for transfers between devices  19.3 us
    psum x1, blocking collectives, local(): force_total = lax.psum(force_local, 'blk')  17.7 us
    ppermute x6, starting transfers between devices, passed_along(): return lax.ppermute(value, axis, pairs)  9.23 us
    reduce_sum x24, other arithmetic, block_terms(): grad_y.sum(axis=1)  9.08 us
    dot_general x24, matrix products, block_terms(): pressure = jnp.dot(kernel, strength, preferred_element_type=jnp.float32)  7.89 us
    dot_general x24, matrix products, block_terms(): lax.dot_general(recv_modes, paired, (((1,), (1,)), ((), ())), preferred_e...  7.17 us
    unnamed x11, local copies, waits for them, and re-layouts  3.97 us
  transfers between devices with their start and end apart: 7, of which 2 were waited for; matrix products, arithmetic and copies ran while one was open for 61% of the time, Pallas kernels for 0%

commit v1 on v0

v1 whole, which is shorter than its diff:
```python
import functools
import math

import jax
import jax.numpy as jnp
from jax import lax
from jax.experimental import pallas as pl
from jax.experimental.pallas import tpu as pltpu
from jax.sharding import PartitionSpec as P

CHORD_SHIFT = 0.5
CORE_SQUARE = 0.25
CHUNK = 256

NN = (((1,), (0,)), ((), ()))
NT = (((1,), (1,)), ((), ()))


def passed_along(value, axis, steps):
    count = lax.axis_size(axis)
    pairs = [(source, (source + steps) % count) for source in range(count)]
    return lax.ppermute(value, axis, pairs)


def product(left, right, dims, precision=None):
    return lax.dot_general(
        left, right, dims, preferred_element_type=jnp.float32, precision=precision
    )


def turned_modes(modes, angle):
    flat = modes.astype(jnp.float32).T
    cols = flat.shape[0] // 4
    cosine = jnp.cos(angle)
    sine = jnp.sin(angle)
    real = [flat[:cols], flat[2 * cols : 3 * cols]]
    imag = [flat[cols : 2 * cols], flat[3 * cols :]]
    parts = []
    for re, im in zip(real, imag):
        parts += [re * cosine - im * sine, re * sine + im * cosine]
    return jnp.concatenate(parts, axis=0)


def halves(value):
    high = value.astype(jnp.bfloat16)
    low = (value - high.astype(jnp.float32)).astype(jnp.bfloat16)
    return high, low


def moment_rows(pos):
    count = pos.shape[1]
    return jnp.concatenate(
        [jnp.ones((1, count), jnp.float32), pos, jnp.zeros((12, count), jnp.float32)], axis=0
    ).astype(jnp.bfloat16)


def tile_kernel(
    offset, table_ref, index_ref, rgeom_ref, rmodes_ref, sgeom_ref, smodes_ref,
    row_ref, col_ref, force_ref, sums_ref, moments_ref, back_ref, backm_ref,
):
    count = rmodes_ref.shape[0]
    cols = rmodes_ref.shape[1] // 4
    wave = table_ref[index_ref[0, offset]]
    rpos = rgeom_ref[...].astype(jnp.float32)
    spos = sgeom_ref[...].astype(jnp.float32)
    recv = turned_modes(rmodes_ref[...], wave * (rpos[0:1] + CHORD_SHIFT))
    send = turned_modes(smodes_ref[...], wave * spos[0:1])
    rhigh, rlow = halves(recv)
    shigh, slow = halves(send)
    rboth = jnp.concatenate([rhigh, rlow], axis=0)
    sboth = jnp.concatenate([shigh, slow], axis=0)
    flipped = jnp.concatenate([shigh[2 * cols :], shigh[: 2 * cols]], axis=0)
    paired = jnp.concatenate([flipped, flipped], axis=0)
    rows = jnp.concatenate([rhigh.T, rlow.T], axis=1)
    rmom = moment_rows(rpos)
    smom = moment_rows(spos)
    place = jnp.concatenate([rpos, jnp.zeros((5, count), jnp.float32)], axis=0).T
    for start in range(0, count, CHUNK):
        part = slice(start, start + CHUNK)
        along = product(rows[part], paired, NN)
        dx = (place[part, 0:1] + CHORD_SHIFT) - spos[0:1]
        dy = place[part, 1:2] - spos[1:2]
        dz = place[part, 2:3] - spos[2:3]
        inverse = lax.rsqrt(dx * dx + dy * dy + (dz * dz + CORE_SQUARE))
        kernel = inverse.astype(jnp.bfloat16)
        cubed = ((inverse * inverse) * (inverse * along)).astype(jnp.bfloat16)
        sums_ref[:, part] = product(sboth, kernel, NT)
        moments_ref[:, part] = product(smom, cubed, NT)
        back = product(rboth[:, part], kernel, NN)
        backm = product(rmom[:, part], cubed, NN)
        if start == 0:
            back_ref[...] = back
            backm_ref[...] = backm
        else:
            back_ref[...] += back
            backm_ref[...] += backm
    full = 4 * cols
    ahead = sums_ref[:full] + sums_ref[full:]
    behind = back_ref[:full] + back_ref[full:]

    def quarter(value, k):
        return value[k * cols : (k + 1) * cols]

    def crossed(left, right):
        terms = (
            quarter(left, 0) * quarter(right, 3)
            - quarter(left, 1) * quarter(right, 2)
            + quarter(left, 2) * quarter(right, 1)
            - quarter(left, 3) * quarter(right, 0)
        )
        return jnp.sum(terms, axis=0, keepdims=True)

    row_turn = wave * crossed(recv, ahead)
    col_turn = wave * crossed(behind, send)
    rm = moments_ref[...]
    sm = backm_ref[...]
    row_ref[0:1] = row_turn - ((rpos[0:1] + CHORD_SHIFT) * rm[0:1] - rm[1:2])
    row_ref[1:2] = rm[2:3] - rpos[1:2] * rm[0:1]
    row_ref[2:3] = rm[3:4] - rpos[2:3] * rm[0:1]
    col_ref[0:1] = (sm[1:2] + CHORD_SHIFT * sm[0:1] - spos[0:1] * sm[0:1]) - col_turn
    col_ref[1:2] = sm[2:3] - spos[1:2] * sm[0:1]
    col_ref[2:3] = sm[3:4] - spos[2:3] * sm[0:1]
    gram = product(recv[: 2 * cols], ahead[2 * cols :], NT, lax.Precision.HIGHEST)
    force_ref[0] = gram[:cols, :cols] + gram[cols:, cols:]
    force_ref[1] = gram[:cols, cols:] - gram[cols:, :cols]


def tile_terms(offset, table, index, rgeom, rmodes, sgeom, smodes):
    count, width = rmodes.shape
    cols = width // 4
    smem = pl.BlockSpec(memory_space=pltpu.SMEM)
    vmem = pl.BlockSpec(memory_space=pltpu.VMEM)
    return pl.pallas_call(
        functools.partial(tile_kernel, offset),
        out_shape=(
            jax.ShapeDtypeStruct((3, count), jnp.float32),
            jax.ShapeDtypeStruct((3, count), jnp.float32),
            jax.ShapeDtypeStruct((2, cols, cols), jnp.float32),
        ),
        in_specs=[smem, smem, vmem, vmem, vmem, vmem],
        out_specs=(vmem, vmem, vmem),
        scratch_shapes=[
            pltpu.VMEM((2 * width, count), jnp.float32),
            pltpu.VMEM((16, count), jnp.float32),
            pltpu.VMEM((2 * width, count), jnp.float32),
            pltpu.VMEM((16, count), jnp.float32),
        ],
        compiler_params=pltpu.CompilerParams(vmem_limit_bytes=48 << 20),
        cost_estimate=pl.CostEstimate(
            flops=2 * count * count * width * 6,
            transcendentals=count * count,
            bytes_accessed=4 * count * width,
        ),
    )(table, index, rgeom, rmodes, sgeom, smodes)


def local(geometry, modes, reduced_freq, freq_index):
    row_count = geometry.shape[1]
    own = modes[0]
    columns = own.shape[1] // 4
    steps = freq_index.shape[1]
    freqs = lax.axis_size("freq")
    sending = [(geometry, own)]
    for _ in range(1, steps):
        sending.append(passed_along(sending[-1], "blk", 1))
    total = 0.0
    force = 0.0
    for offset in range(steps):
        row, col, part = tile_terms(
            offset, reduced_freq, freq_index, geometry, own, *sending[offset]
        )
        back = passed_along(col, "blk", -offset) if offset else col
        total = total + row + back
        force = force + part
    grad_scale = 1.0 / math.sqrt(columns * steps * row_count * freqs)
    force_scale = 1.0 / math.sqrt(row_count * row_count * lax.axis_size("blk") * steps)
    share = row_count // freqs
    mine = lax.axis_index("freq")
    pieces = total * grad_scale
    result = lax.psum_scatter(pieces[None], "freq", scatter_dimension=2, tiled=True)[0]
    force_total = lax.psum(force * force_scale, "blk")
    return (result, force_total[None])


def solution(mesh):
    return jax.shard_map(
        local,
        mesh=mesh,
        in_specs=(
            P(None, ("case", "blk")),
            P("freq", ("case", "blk"), None),
            P(),
            P(("case", "freq"), None),
        ),
        out_specs=(P(None, ("case", "blk", "freq")), P(("case", "freq"), None, None, None)),
        check_vma=False,
    )
```

time: 178 us -> 81.4 us (0.46)
  other arithmetic: 91.4 us -> 0.03 us
  matrix products: 16.2 us -> 0 us
  Pallas kernels: 0 us -> 15.4 us
    another operation x25 -> x0, other arithmetic: 76.2 us -> none
    dot_general x52 -> x0, matrix products: 16.2 us -> none  [the longest x24 7.89 us: block_terms(): pressure = jnp.dot(kernel, strength, preferred_element_type=jnp.float32)]
    pallas_call x0 -> x3, Pallas kernels: none -> 15.4 us  [tile_terms(): pl.pallas_call(functools.partial(tile_kernel, offset), out_shape=(jax.Sha...]
    unnamed x2, waiting for transfers between devices: 19.3 us -> 5.2 us
    ppermute x6, waiting for transfers between devices: 3.04 us -> 16.8 us  [passed_along(): return lax.ppermute(value, axis, pairs)]
    reduce_sum x25 -> x0, other arithmetic: 9.26 us -> none  [the longest x24 9.08 us: block_terms(): grad_y.sum(axis=1)]
    neg x3 -> x0, other arithmetic: 2.25 us -> none  [prepare_sender(): -send_modes[:, 3 * columns:]]
    concatenate x6 -> x0, other arithmetic: 2.09 us -> none  [the longest x3 1.5 us: prepare_sender(): paired = jnp.concatenate([flipped, turned], axis=0)]
  transfers between devices with their start and end apart: 7 -> 7, of which waited for: 2 -> 3; matrix products, arithmetic and copies ran while one was open for 61% -> 0% of each run, Pallas kernels for 0% -> 19%
where the time goes in v1:
time: 81.4 us; the launch traced here: 81.2 us
  waiting for transfers between devices  22 us (27%)
  blocking collectives  16.9 us (21%)
  Pallas kernels  15.4 us (19%)
  between operations  14.1 us (17%)
  starting transfers between devices  8.53 us (10%)
  local copies, waits for them, and re-layouts  4.26 us (5%)
    psum x1, blocking collectives, local(): force_total = lax.psum(force * force_scale, 'blk')  16.9 us
    ppermute x6, waiting for transfers between devices, passed_along(): return lax.ppermute(value, axis, pairs)  16.8 us
    pallas_call x3, Pallas kernels, tile_terms(): pl.pallas_call(functools.partial(tile_kernel, offset), out_shape=(jax.Sha...  15.4 us
    ppermute x6, starting transfers between devices, passed_along(): return lax.ppermute(value, axis, pairs)  8.49 us
    unnamed x2, waiting for transfers between devices  5.2 us
    unnamed x10, local copies, waits for them, and re-layouts  4.26 us
  transfers between devices with their start and end apart: 7, of which 3 were waited for; matrix products, arithmetic and copies ran while one was open for 0% of the time, Pallas kernels for 19%

profile of v1, /device:TPU:0, one launch (start us, length us, event | category | flops | bytes accessed | tf_op | source)
XLA Modules:
  0.0 81.2 jit_solution(10803979323127356583)
XLA Ops:
  7.2 0.0 copy-start.3
  7.2 0.0 copy-start.2
  7.2 0.0 reduce-scatter.4.cloned.1.call-start
  7.2 3.1 %collective-permute-start.1 = (bf16[1024,128]{1,0:T(8,128)(2,1)}, bf16[1024,128]{1,0:T(8,128)(2,1)S(1)}, u32[]{:S(2)}, u32[]{:S(2)}) collective-permute-start(bf16[1024,128]{1,0:T(8,128)(2,1)} %bitcast.12), channel_id=1, source_target_pairs={{0,4},{4,8},{8,12},{12,0},{1,5},{5,9},{9,13},{13,1},{2,6},{6,10},{... | collective-permute-start | bytes 786440 | tf_op jit(solution)/shard_map/ppermute | solution.py:22
  10.3 8.5 %collective-permute-done.1.smodes_ref = bf16[1024,128]{1,0:T(8,128)(2,1)S(1)} collective-permute-done((bf16[1024,128]{1,0:T(8,128)(2,1)}, bf16[1024,128]{1,0:T(8,128)(2,1)S(1)}, u32[]{:S(2)}, u32[]{:S(2)}) %collective-permute-start.1) | collective-permute-done | bytes 262176 | tf_op jit(solution)/shard_map/ppermute | solution.py:22
  18.8 0.0 collective-permute-start.4
  18.9 1.3 %collective-permute-start = (bf16[3,1024]{1,0:T(4,128)(2,1)}, bf16[3,1024]{1,0:T(4,128)(2,1)S(1)}, u32[]{:S(2)}, u32[]{:S(2)}) collective-permute-start(bf16[3,1024]{1,0:T(4,128)(2,1)} %rgeom_ref.5), channel_id=1, source_target_pairs={{0,4},{4,8},{8,12},{12,0},{1,5},{5,9},{9,13},{13,1},{2,6},{6,10},{... | collective-permute-start | bytes 18440 | tf_op jit(solution)/shard_map/ppermute | solution.py:22
  20.1 8.2 %collective-permute-done.sgeom_ref = bf16[3,1024]{1,0:T(4,128)(2,1)S(1)} collective-permute-done((bf16[3,1024]{1,0:T(4,128)(2,1)}, bf16[3,1024]{1,0:T(4,128)(2,1)S(1)}, u32[]{:S(2)}, u32[]{:S(2)}) %collective-permute-start) | collective-permute-done | bytes 6176 | tf_op jit(solution)/shard_map/ppermute | solution.py:22
  28.3 0.0 collective-permute-start.3
  28.3 0.0 copy-done.3
  28.3 0.0 copy-done.2
  28.3 0.0 copy-start
  28.3 0.9 %copy-done = bf16[1,1024,128]{2,1,0:T(8,128)(2,1)S(1)} copy-done((bf16[1,1024,128]{2,1,0:T(8,128)(2,1)S(1)}, bf16[1,1024,128]{2,1,0:T(8,128)(2,1)}, u32[]{:S(2)}) %copy-start) | copy-done | bytes 262168
  29.3 0.0 copy-start.1
  29.3 0.7 copy-done.1
  30.0 5.1 %shard_map.60 = (f32[3,1024]{1,0:T(4,128)S(1)}, f32[3,1024]{1,0:T(4,128)S(1)}, f32[2,32,32]{2,1,0:T(8,128)S(1)}) custom-call(f32[16]{0:T(128)S(1)} %copy-done.2, s32[1,3]{1,0:T(1,128)S(1)} %copy-done.3, bf16[3,1024]{1,0:T(4,128)(2,1)S(1)} %copy-done.1, bf16[1024,128]{1,0:T(8,128)(2,1)S(1)} %bitcast.13, bf16[3,1024]{1,0:T(4,128)(2,1)S(1)} %collective-permute-done.sgeom_ref, ...), custom_call_target="tpu_custom_call" | custom-call | flops 1610612736 | bytes 524288 | tf_op jit(solution)/shard_map/pallas_call | solution.py:133
  35.1 4.0 %collective-permute-start.2 = (f32[3,1024]{1,0:T(4,128)S(1)}, f32[3,1024]{1,0:T(4,128)S(1)}, u32[]{:S(2)}, u32[]{:S(2)}) collective-permute-start(f32[3,1024]{1,0:T(4,128)S(1)} %get-tuple-element.14), channel_id=1, source_target_pairs={{0,12},{4,0},{8,4},{12,8},{1,13},{5,1},{9,5},{13,9},{2,14},{6,2},{... | collective-permute-start | bytes 36872 | tf_op jit(solution)/shard_map/ppermute | solution.py:22
  39.2 0.0 collective-permute-done.3.sgeom_ref
  39.2 0.0 collective-permute-done.4.smodes_ref
  39.2 5.1 %shard_map.61 = (f32[3,1024]{1,0:T(4,128)S(1)}, f32[3,1024]{1,0:T(4,128)S(1)}, f32[2,32,32]{2,1,0:T(8,128)S(1)}) custom-call(f32[16]{0:T(128)S(1)} %copy-done.2, s32[1,3]{1,0:T(1,128)S(1)} %copy-done.3, bf16[3,1024]{1,0:T(4,128)(2,1)S(1)} %copy-done.1, bf16[1024,128]{1,0:T(8,128)(2,1)S(1)} %bitcast.14, bf16[3,1024]{1,0:T(4,128)(2,1)S(1)} %collective-permute-done.3.sgeom_ref, ...), custom_call_target="tpu_custom_call" | custom-call | flops 1610612736 | bytes 524288 | tf_op jit(solution)/shard_map/pallas_call | solution.py:133
  44.3 0.1 collective-permute-start.5
  44.4 5.1 %shard_map.59 = (f32[3,1024]{1,0:T(4,128)S(1)}, f32[3,1024]{1,0:T(4,128)S(1)}, f32[2,32,32]{2,1,0:T(8,128)S(1)}) custom-call(f32[16]{0:T(128)S(1)} %copy-done.2, s32[1,3]{1,0:T(1,128)S(1)} %copy-done.3, bf16[3,1024]{1,0:T(4,128)(2,1)S(1)} %copy-done.1, bf16[1024,128]{1,0:T(8,128)(2,1)S(1)} %bitcast.15, bf16[3,1024]{1,0:T(4,128)(2,1)S(1)} %copy-done.1, ...), custom_call_target="tpu_custom_call" | custom-call | flops 1610612736 | bytes 524288 | tf_op jit(solution)/shard_map/pallas_call | solution.py:133
  49.5 0.0 collective-permute-done.2
  49.5 0.0 collective-permute-done.5
  49.6 1.0 %copy.6 = f32[1,3,1024]{1,0,2:T(1,128)} copy(f32[1,3,1024]{2,1,0:T(4,128)S(1)} %multiply_bitcast_fusion.1) | data formatting | bytes 24576
  50.6 0.0 reduce-scatter.4.cloned.1.call-update
  50.7 16.9 %psum.7 = f32[1,2,32,32]{3,2,1,0:T(8,128)} all-reduce(f32[1,2,32,32]{3,2,1,0:T(8,128)S(1)} %multiply_bitcast_fusion), channel_id=1, replica_groups=mesh['case'=2,'blk'=4,'freq'=4] {'blk'}, use_global_device_ids=true, to_apply=%region_1.0 | all-reduce | flops 2048 | bytes 16384 | tf_op jit(solution)/shard_map/psum | solution.py:181
  67.6 5.2 %reduce-scatter.4.cloned.1.call-done = f32[256,3]{1,0:T(8,128)} async-done(((f32[1024,3]{1,0:T(8,128)}), f32[256,3]{1,0:T(8,128)}) %reduce-scatter.4.cloned.1.call-update) | async-done | bytes 3088
  72.8 1.6 %copy.7 = f32[1,3,256]{2,1,0:T(4,128)} copy(f32[1,3,256]{1,0,2:T(1,128)} %bitcast.18) | data formatting | bytes 6144
  (2 shorter events, 0.0 us)
Async XLA Ops:
  7.2 21.2 %copy-start.3 = (s32[1,3]{1,0:T(1,128)S(1)}, s32[1,3]{1,0:T(1,128)}, u32[]{:S(2)}) copy-start(s32[1,3]{1,0:T(1,128)} %index_ref.5) | copy-start | bytes 40
  7.2 21.1 %copy-start.2 = (f32[16]{0:T(128)S(1)}, f32[16]{0:T(128)}, u32[]{:S(2)}) copy-start(f32[16]{0:T(128)} %table_ref.5) | copy-start | bytes 196
  7.2 65.6 %reduce-scatter.4.cloned.1.call-start = ((), (), s32[]{:S(2)}) async-start(), calls=%async_computation.1 | async-start | bytes 655360
  7.2 11.6 %collective-permute-start.1 = (bf16[1024,128]{1,0:T(8,128)(2,1)}, bf16[1024,128]{1,0:T(8,128)(2,1)S(1)}, u32[]{:S(2)}, u32[]{:S(2)}) collective-permute-start(bf16[1024,128]{1,0:T(8,128)(2,1)} %bitcast.12), channel_id=1, source_target_pairs={{0,4},{4,8},{8,12},{12,0},{1,5},{5,9},{9,13},{13,1},{2,6},{6,10},{... | collective-permute-start | bytes 786440 | tf_op jit(solution)/shard_map/ppermute | solution.py:22
  18.8 20.3 %collective-permute-start.4 = (bf16[1024,128]{1,0:T(8,128)(2,1)S(1)}, bf16[1024,128]{1,0:T(8,128)(2,1)S(1)}, u32[]{:S(2)}, u32[]{:S(2)}) collective-permute-start(bf16[1024,128]{1,0:T(8,128)(2,1)S(1)} %collective-permute-done.1.smodes_ref), channel_id=1, source_target_pairs={{0,4},{4,8},{8,12},{12,0},{1,5},{5,9},{9,13},{13,1},{2,6},{6,10},{... | collective-permute-start | bytes 786440 | tf_op jit(solution)/shard_map/ppermute | solution.py:22
  18.9 9.5 %collective-permute-start = (bf16[3,1024]{1,0:T(4,128)(2,1)}, bf16[3,1024]{1,0:T(4,128)(2,1)S(1)}, u32[]{:S(2)}, u32[]{:S(2)}) collective-permute-start(bf16[3,1024]{1,0:T(4,128)(2,1)} %rgeom_ref.5), channel_id=1, source_target_pairs={{0,4},{4,8},{8,12},{12,0},{1,5},{5,9},{9,13},{13,1},{2,6},{6,10},{... | collective-permute-start | bytes 18440 | tf_op jit(solution)/shard_map/ppermute | solution.py:22
  28.3 10.8 %collective-permute-start.3 = (bf16[3,1024]{1,0:T(4,128)(2,1)S(1)}, bf16[3,1024]{1,0:T(4,128)(2,1)S(1)}, u32[]{:S(2)}, u32[]{:S(2)}) collective-permute-start(bf16[3,1024]{1,0:T(4,128)(2,1)S(1)} %collective-permute-done.sgeom_ref), channel_id=1, source_target_pairs={{0,4},{4,8},{8,12},{12,0},{1,5},{5,9},{9,13},{13,1},{2,6},{6,10},{... | collective-permute-start | bytes 18440 | tf_op jit(solution)/shard_map/ppermute | solution.py:22
  28.3 1.0 %copy-start = (bf16[1,1024,128]{2,1,0:T(8,128)(2,1)S(1)}, bf16[1,1024,128]{2,1,0:T(8,128)(2,1)}, u32[]{:S(2)}) copy-start(bf16[1,1024,128]{2,1,0:T(8,128)(2,1)} %param.5) | copy-start | bytes 786436
  29.3 0.7 copy-start.1
  35.1 14.4 %collective-permute-start.2 = (f32[3,1024]{1,0:T(4,128)S(1)}, f32[3,1024]{1,0:T(4,128)S(1)}, u32[]{:S(2)}, u32[]{:S(2)}) collective-permute-start(f32[3,1024]{1,0:T(4,128)S(1)} %get-tuple-element.14), channel_id=1, source_target_pairs={{0,12},{4,0},{8,4},{12,8},{1,13},{5,1},{9,5},{13,9},{2,14},{6,2},{... | collective-permute-start | bytes 36872 | tf_op jit(solution)/shard_map/ppermute | solution.py:22
  44.3 5.3 %collective-permute-start.5 = (f32[3,1024]{1,0:T(4,128)S(1)}, f32[3,1024]{1,0:T(4,128)S(1)}, u32[]{:S(2)}, u32[]{:S(2)}) collective-permute-start(f32[3,1024]{1,0:T(4,128)S(1)} %get-tuple-element.16), channel_id=1, source_target_pairs={{0,8},{4,12},{8,0},{12,4},{1,9},{5,13},{9,1},{13,5},{2,10},{6,14},... | collective-permute-start | bytes 36872 | tf_op jit(solution)/shard_map/ppermute | solution.py:22
Sparse Core Ops, SparseCore 0:
  50.8 21.9 reduce-scatter.3

commit v2 on v1

--- a/solution.py
+++ b/solution.py
@@ -55,9 +55,11 @@
 
 
 def tile_kernel(
-    offset, table_ref, index_ref, rgeom_ref, rmodes_ref, sgeom_ref, smodes_ref,
-    row_ref, col_ref, force_ref, sums_ref, moments_ref, back_ref, backm_ref,
+    offset, plan, table_ref, index_ref, rgeom_ref, rmodes_ref, sgeom_ref, smodes_ref, *refs
 ):
+    held = refs[: plan.held]
+    grads = refs[plan.held : plan.held + plan.grads]
+    force_ref, sums_ref, moments_ref, back_ref, backm_ref = refs[plan.held + plan.grads :]
     count = rmodes_ref.shape[0]
     cols = rmodes_ref.shape[1] // 4
     wave = table_ref[index_ref[0, offset]]
@@ -114,71 +116,115 @@
     col_turn = wave * crossed(behind, send)
     rm = moments_ref[...]
     sm = backm_ref[...]
-    row_ref[0:1] = row_turn - ((rpos[0:1] + CHORD_SHIFT) * rm[0:1] - rm[1:2])
-    row_ref[1:2] = rm[2:3] - rpos[1:2] * rm[0:1]
-    row_ref[2:3] = rm[3:4] - rpos[2:3] * rm[0:1]
-    col_ref[0:1] = (sm[1:2] + CHORD_SHIFT * sm[0:1] - spos[0:1] * sm[0:1]) - col_turn
-    col_ref[1:2] = sm[2:3] - spos[1:2] * sm[0:1]
-    col_ref[2:3] = sm[3:4] - spos[2:3] * sm[0:1]
+    row = jnp.concatenate(
+        [
+            row_turn - ((rpos[0:1] + CHORD_SHIFT) * rm[0:1] - rm[1:2]),
+            rm[2:3] - rpos[1:2] * rm[0:1],
+            rm[3:4] - rpos[2:3] * rm[0:1],
+        ],
+        axis=0,
+    )
+    col = jnp.concatenate(
+        [
+            (sm[1:2] + CHORD_SHIFT * sm[0:1] - spos[0:1] * sm[0:1]) - col_turn,
+            sm[2:3] - spos[1:2] * sm[0:1],
+            sm[3:4] - spos[2:3] * sm[0:1],
+        ],
+        axis=0,
+    )
     gram = product(recv[: 2 * cols], ahead[2 * cols :], NT, lax.Precision.HIGHEST)
-    force_ref[0] = gram[:cols, :cols] + gram[cols:, cols:]
-    force_ref[1] = gram[:cols, cols:] - gram[cols:, :cols]
-
-
-def tile_terms(offset, table, index, rgeom, rmodes, sgeom, smodes):
-    count, width = rmodes.shape
+    force_real = (gram[:cols, :cols] + gram[cols:, cols:]) * plan.force_scale
+    force_imag = (gram[:cols, cols:] - gram[cols:, :cols]) * plan.force_scale
+    row = row * plan.grad_scale
+    col = col * plan.grad_scale
+    if plan.role == "own":
+        grads[0][...] = row + col
+        force_ref[0] = force_real
+        force_ref[1] = force_imag
+    elif plan.role == "below":
+        grads[0][...] = held[0][...] + row
+        grads[1][...] = col
+        force_ref[0] = held[1][0] + force_real
+        force_ref[1] = held[1][1] + force_imag
+    else:
+        grads[0][...] = row
+        grads[1][...] = held[0][...] + col
+        force_ref[0] = held[1][0] + force_real
+        force_ref[1] = held[1][1] + force_imag
+
+
+class Plan:
+    def __init__(self, role, grad_scale, force_scale):
+        self.role = role
+        self.grad_scale = grad_scale
+        self.force_scale = force_scale
+        self.held = 0 if role == "own" else 2
+        self.grads = 1 if role == "own" else 2
+
+
+def tile_terms(offset, plan, table, index, recv, send, *held):
+    count, width = recv[1].shape
     cols = width // 4
     smem = pl.BlockSpec(memory_space=pltpu.SMEM)
     vmem = pl.BlockSpec(memory_space=pltpu.VMEM)
+    grad = jax.ShapeDtypeStruct((3, count), jnp.float32)
+    force = jax.ShapeDtypeStruct((2, cols, cols), jnp.float32)
     return pl.pallas_call(
-        functools.partial(tile_kernel, offset),
-        out_shape=(
-            jax.ShapeDtypeStruct((3, count), jnp.float32),
-            jax.ShapeDtypeStruct((3, count), jnp.float32),
-            jax.ShapeDtypeStruct((2, cols, cols), jnp.float32),
-        ),
-        in_specs=[smem, smem, vmem, vmem, vmem, vmem],
-        out_specs=(vmem, vmem, vmem),
+        functools.partial(tile_kernel, offset, plan),
+        out_shape=(grad,) * plan.grads + (force,),
+        in_specs=[smem, smem] + [vmem] * (4 + plan.held),
+        out_specs=(vmem,) * (plan.grads + 1),
         scratch_shapes=[
             pltpu.VMEM((2 * width, count), jnp.float32),
             pltpu.VMEM((16, count), jnp.float32),
             pltpu.VMEM((2 * width, count), jnp.float32),
             pltpu.VMEM((16, count), jnp.float32),
         ],
+        name="tile_" + plan.role,
         compiler_params=pltpu.CompilerParams(vmem_limit_bytes=48 << 20),
         cost_estimate=pl.CostEstimate(
             flops=2 * count * count * width * 6,
             transcendentals=count * count,
             bytes_accessed=4 * count * width,
         ),
-    )(table, index, rgeom, rmodes, sgeom, smodes)
+    )(table, index, *recv, *send, *held)
 
 
 def local(geometry, modes, reduced_freq, freq_index):
     row_count = geometry.shape[1]
-    own = modes[0]
-    columns = own.shape[1] // 4
+    own = (geometry, modes[0])
+    columns = modes.shape[2] // 4
     steps = freq_index.shape[1]
+    blocks = lax.axis_size("blk")
     freqs = lax.axis_size("freq")
-    sending = [(geometry, own)]
-    for _ in range(1, steps):
-        sending.append(passed_along(sending[-1], "blk", 1))
-    total = 0.0
-    force = 0.0
-    for offset in range(steps):
-        row, col, part = tile_terms(
-            offset, reduced_freq, freq_index, geometry, own, *sending[offset]
-        )
-        back = passed_along(col, "blk", -offset) if offset else col
-        total = total + row + back
-        force = force + part
     grad_scale = 1.0 / math.sqrt(columns * steps * row_count * freqs)
-    force_scale = 1.0 / math.sqrt(row_count * row_count * lax.axis_size("blk") * steps)
+    force_scale = 1.0 / math.sqrt(row_count * row_count * blocks * steps)
+    below = passed_along(own, "blk", 1)
+    above = passed_along(own, "blk", -1)
+    def terms(offset, role, *operands):
+        plan = Plan(role, grad_scale, force_scale)
+        return tile_terms(offset, plan, reduced_freq, freq_index, *operands)
+
+    mine, force = terms(0, "own", own, own)
+    mine, down, force = terms(1, "below", own, below, mine, force)
+    up, down, force = terms(2, "across", above, below, down, force)
+    total = mine + passed_along(down, "blk", -1) + passed_along(up, "blk", 1)
+    if blocks == 4:
+        force_total = force
+        for shift in (-1, 1, 2):
+            force_total = force_total + passed_along(force, "blk", shift)
+    else:
+        force_total = lax.psum(force, "blk")
     share = row_count // freqs
-    mine = lax.axis_index("freq")
-    pieces = total * grad_scale
-    result = lax.psum_scatter(pieces[None], "freq", scatter_dimension=2, tiled=True)[0]
-    force_total = lax.psum(force * force_scale, "blk")
+    place = lax.axis_index("freq")
+    result = None
+    for flip in range(freqs):
+        piece = lax.dynamic_slice_in_dim(total, (place ^ flip) * share, share, axis=1)
+        if flip:
+            pairs = [(source, source ^ flip) for source in range(freqs)]
+            result = result + lax.ppermute(piece, "freq", pairs)
+        else:
+            result = piece
     return (result, force_total[None])
 
 

time: 81.4 us -> 41.4 us (0.51)
  waiting for transfers between devices: 22 us -> 5.02 us
  blocking collectives: 16.9 us -> 0 us
  between operations: 14.1 us -> 0.7 us
  starting transfers between devices: 8.53 us -> 17 us
  local copies, waits for them, and re-layouts: 4.26 us -> 1.67 us
  other arithmetic: 0.03 us -> 1.23 us
    psum x1 -> x0, blocking collectives: 16.9 us -> none  [local(): force_total = lax.psum(force * force_scale, 'blk')]
    ppermute x6 -> x9, waiting for transfers between devices: 16.8 us -> 3.71 us  [passed_along(): return lax.ppermute(value, axis, pairs)]
    ppermute x6 -> x9, starting transfers between devices: 8.49 us -> 15.1 us  [passed_along(): return lax.ppermute(value, axis, pairs)]
    unnamed x2 -> x0, waiting for transfers between devices: 5.2 us -> none
    unnamed x10 -> x8, local copies, waits for them, and re-layouts: 4.26 us -> 1.66 us
    ppermute x0 -> x3, starting transfers between devices: none -> 1.93 us  [local(): result = result + lax.ppermute(piece, 'freq', pairs)]
    ppermute x0 -> x3, waiting for transfers between devices: none -> 1.31 us  [local(): result = result + lax.ppermute(piece, 'freq', pairs)]
  transfers between devices with their start and end apart: 7 -> 12, of which waited for: 3 -> 5; matrix products, arithmetic and copies ran while one was open for 0% -> 2% of each run, Pallas kernels for 19% -> 25%
where the time goes in v2:
time: 41.4 us; the launch traced here: 41.2 us
  starting transfers between devices  17 us (41%)
  Pallas kernels  15.5 us (37%)
  waiting for transfers between devices  5.02 us (12%)
  local copies, waits for them, and re-layouts  1.67 us (4%)
  other arithmetic  1.23 us (3%)
  between operations  0.7 us (2%)
    pallas_call x3, Pallas kernels, tile_terms(): pl.pallas_call(functools.partial(tile_kernel, offset, plan), out_shape=(g...  15.5 us
    ppermute x9, starting transfers between devices, passed_along(): return lax.ppermute(value, axis, pairs)  15.1 us
    ppermute x9, waiting for transfers between devices, passed_along(): return lax.ppermute(value, axis, pairs)  3.71 us
    ppermute x3, starting transfers between devices, local(): result = result + lax.ppermute(piece, 'freq', pairs)  1.93 us
    unnamed x8, local copies, waits for them, and re-layouts  1.66 us
    ppermute x3, waiting for transfers between devices, local(): result = result + lax.ppermute(piece, 'freq', pairs)  1.31 us
  transfers between devices with their start and end apart: 12, of which 5 were waited for; matrix products, arithmetic and copies ran while one was open for 2% of the time, Pallas kernels for 25%

profile of v2, /device:TPU:0, one launch (start us, length us, event | category | flops | bytes accessed | tf_op | source)
XLA Modules:
  0.0 41.2 jit_solution(16233307736001037308)
XLA Ops:
  0.6 0.0 copy-start.2
  0.6 0.0 copy-start.3
  0.7 3.1 %collective-permute-start.1 = (bf16[1024,128]{1,0:T(8,128)(2,1)}, bf16[1024,128]{1,0:T(8,128)(2,1)S(1)}, u32[]{:S(2)}, u32[]{:S(2)}) collective-permute-start(bf16[1024,128]{1,0:T(8,128)(2,1)} %bitcast.3), channel_id=1, source_target_pairs={{0,4},{4,8},{8,12},{12,0},{1,5},{5,9},{9,13},{13,1},{2,6},{6,10},{... | collective-permute-start | bytes 786440 | tf_op jit(solution)/shard_map/ppermute | solution.py:22
  3.7 2.1 %collective-permute-start.3 = (bf16[1024,128]{1,0:T(8,128)(2,1)}, bf16[1024,128]{1,0:T(8,128)(2,1)S(1)}, u32[]{:S(2)}, u32[]{:S(2)}) collective-permute-start(bf16[1024,128]{1,0:T(8,128)(2,1)} %bitcast.4), channel_id=1, source_target_pairs={{0,12},{4,0},{8,4},{12,8},{1,13},{5,1},{9,5},{13,9},{2,14},{6,2},{... | collective-permute-start | bytes 786440 | tf_op jit(solution)/shard_map/ppermute | solution.py:22
  5.8 0.0 collective-permute-start
  5.8 3.8 %collective-permute-start.2 = (bf16[3,1024]{1,0:T(4,128)(2,1)}, bf16[3,1024]{1,0:T(4,128)(2,1)S(1)}, u32[]{:S(2)}, u32[]{:S(2)}) collective-permute-start(bf16[3,1024]{1,0:T(4,128)(2,1)} %rgeom_ref.3), channel_id=1, source_target_pairs={{0,12},{4,0},{8,4},{12,8},{1,13},{5,1},{9,5},{13,9},{2,14},{6,2},{... | collective-permute-start | bytes 18440 | tf_op jit(solution)/shard_map/ppermute | solution.py:22
  9.6 0.0 copy-done.2
  9.6 0.0 copy-done.3
  9.6 0.0 copy-start
  9.7 0.9 %copy-done = bf16[1,1024,128]{2,1,0:T(8,128)(2,1)S(1)} copy-done((bf16[1,1024,128]{2,1,0:T(8,128)(2,1)S(1)}, bf16[1,1024,128]{2,1,0:T(8,128)(2,1)}, u32[]{:S(2)}) %copy-start) | copy-done | bytes 262168
  10.6 0.0 copy-start.1
  10.6 0.7 %copy-done.1 = bf16[3,1024]{1,0:T(4,128)(2,1)S(1)} copy-done((bf16[3,1024]{1,0:T(4,128)(2,1)S(1)}, bf16[3,1024]{1,0:T(4,128)(2,1)}, u32[]{:S(2)}) %copy-start.1) | copy-done | bytes 6168
  11.3 5.2 %tile_own.1 = (f32[3,1024]{1,0:T(4,128)S(1)}, f32[2,32,32]{2,1,0:T(8,128)S(1)}) custom-call(f32[16]{0:T(128)S(1)} %copy-done.2, s32[1,3]{1,0:T(1,128)S(1)} %copy-done.3, bf16[3,1024]{1,0:T(4,128)(2,1)S(1)} %copy-done.1, bf16[1024,128]{1,0:T(8,128)(2,1)S(1)} %bitcast.5, bf16[3,1024]{1,0:T(4,128)(2,1)S(1)} %copy-done.1, bf16[1024,128]{1,0:T(8,128)(2,1)S(1)} %bitcast.6), custom_call_target="tpu_custom_call" | custom-call | flops 1610612736 | bytes 524288 | tf_op jit(solution)/shard_map/tile_own/pallas_call | solution.py:172
  16.5 1.8 %collective-permute-done.sgeom_ref = bf16[3,1024]{1,0:T(4,128)(2,1)S(1)} collective-permute-done((bf16[3,1024]{1,0:T(4,128)(2,1)}, bf16[3,1024]{1,0:T(4,128)(2,1)S(1)}, u32[]{:S(2)}, u32[]{:S(2)}) %collective-permute-start) | collective-permute-done | bytes 6176 | tf_op jit(solution)/shard_map/ppermute | solution.py:22
  18.2 0.0 collective-permute-done.1.smodes_ref
  18.2 5.2 %tile_below.1 = (f32[3,1024]{1,0:T(4,128)S(1)}, f32[3,1024]{1,0:T(4,128)S(1)}, f32[2,32,32]{2,1,0:T(8,128)S(1)}) custom-call(f32[16]{0:T(128)S(1)} %copy-done.2, s32[1,3]{1,0:T(1,128)S(1)} %copy-done.3, bf16[3,1024]{1,0:T(4,128)(2,1)S(1)} %copy-done.1, bf16[1024,128]{1,0:T(8,128)(2,1)S(1)} %bitcast.7, bf16[3,1024]{1,0:T(4,128)(2,1)S(1)} %collective-permute-done.sgeom_ref, ...), custom_call_target="tpu_custom_call" | custom-call | flops 1610612736 | bytes 524288 | tf_op jit(solution)/shard_map/tile_below/pallas_call | solution.py:172
  23.4 0.0 collective-permute-done.2.rgeom_ref
  23.4 0.0 collective-permute-done.3.rmodes_ref
  23.4 5.2 %tile_across.1 = (f32[3,1024]{1,0:T(4,128)S(1)}, f32[3,1024]{1,0:T(4,128)S(1)}, f32[2,32,32]{2,1,0:T(8,128)S(1)}) custom-call(f32[16]{0:T(128)S(1)} %copy-done.2, s32[1,3]{1,0:T(1,128)S(1)} %copy-done.3, bf16[3,1024]{1,0:T(4,128)(2,1)S(1)} %collective-permute-done.2.rgeom_ref, bf16[1024,128]{1,0:T(8,128)(2,1)S(1)} %collective-permute-done.3.rmodes_ref, ...), custom_call_target="tpu_custom_call" | custom-call | flops 1610612736 | bytes 524288 | tf_op jit(solution)/shard_map/tile_across/pallas_call | solution.py:172
  28.6 1.7 %collective-permute-start.4 = (f32[3,1024]{1,0:T(4,128)S(1)}, f32[3,1024]{1,0:T(4,128)S(1)}, u32[]{:S(2)}, u32[]{:S(2)}) collective-permute-start(f32[3,1024]{1,0:T(4,128)S(1)} %get-tuple-element.15), channel_id=1, source_target_pairs={{0,12},{4,0},{8,4},{12,8},{1,13},{5,1},{9,5},{13,9},{2,14},{6,2},{... | collective-permute-start | bytes 36872 | tf_op jit(solution)/shard_map/ppermute | solution.py:22
  30.4 0.3 collective-permute-start.5
  30.7 0.0 collective-permute-start.10
  30.7 4.1 %collective-permute-start.11 = (f32[2,32,32]{2,1,0:T(8,128)S(1)}, f32[2,32,32]{2,1,0:T(8,128)S(1)}, u32[]{:S(2)}, u32[]{:S(2)}) collective-permute-start(f32[2,32,32]{2,1,0:T(8,128)S(1)} %get-tuple-element.17), channel_id=1, source_target_pairs={{0,8},{4,12},{8,0},{12,4},{1,9},{5,13},{9,1},{13,5},{2,10},{6,14},... | collective-permute-start | bytes 24584 | tf_op jit(solution)/shard_map/ppermute | solution.py:22
  34.8 0.0 collective-permute-start.9
  34.8 0.0 collective-permute-done.4
  34.8 1.1 %collective-permute-done.5 = f32[3,1024]{1,0:T(4,128)S(1)} collective-permute-done((f32[3,1024]{1,0:T(4,128)S(1)}, f32[3,1024]{1,0:T(4,128)S(1)}, u32[]{:S(2)}, u32[]{:S(2)}) %collective-permute-start.5) | collective-permute-done | bytes 12320 | tf_op jit(solution)/shard_map/ppermute | solution.py:22
  35.9 0.1 collective-permute-start.6
  36.0 1.6 %collective-permute-start.7 = (f32[3,256]{1,0:T(4,128)S(1)}, f32[3,256]{1,0:T(4,128)S(1)}, u32[]{:S(2)}, u32[]{:S(2)}) collective-permute-start(f32[3,256]{1,0:T(4,128)S(1)} %get-tuple-element.20), channel_id=1, source_target_pairs={{0,2},{1,3},{2,0},{3,1},{4,6},{5,7},{6,4},{7,5},{8,10},{9,11},{10,... | collective-permute-start | bytes 9224 | tf_op jit(solution)/shard_map/ppermute | solution.py:225
  37.6 0.0 collective-permute-done.10
  37.6 0.3 collective-permute-start.8
  37.9 0.0 collective-permute-done.11
  37.9 0.8 %collective-permute-done.9 = f32[2,32,32]{2,1,0:T(8,128)S(1)} collective-permute-done((f32[2,32,32]{2,1,0:T(8,128)S(1)}, f32[2,32,32]{2,1,0:T(8,128)S(1)}, u32[]{:S(2)}, u32[]{:S(2)}) %collective-permute-start.9) | collective-permute-done | bytes 8224 | tf_op jit(solution)/shard_map/ppermute | solution.py:22
  38.7 0.6 %add_bitcast_fusion = f32[1,2,32,32]{3,2,1,0:T(8,128)} fusion(f32[2,32,32]{2,1,0:T(8,128)S(1)} %collective-permute-done.11, f32[2,32,32]{2,1,0:T(8,128)S(1)} %collective-permute-done.10, f32[2,32,32]{2,1,0:T(8,128)S(1)} %get-tuple-element.17, f32[2,32,32]{2,1,0:T(8,128)S(1)} %collective-permute-done.9), kind=kLoop, calls=%fused_computation | loop fusion | flops 6144 | bytes 40960 | tf_op jit(solution)/shard_map/broadcast_in_dim | solution.py:228
  39.3 0.0 collective-permute-done.6
  39.3 0.4 collective-permute-done.7
  39.7 0.9 %collective-permute-done.8 = f32[3,256]{1,0:T(4,128)S(1)} collective-permute-done((f32[3,256]{1,0:T(4,128)S(1)}, f32[3,256]{1,0:T(4,128)S(1)}, u32[]{:S(2)}, u32[]{:S(2)}) %collective-permute-start.8) | collective-permute-done | bytes 3104 | tf_op jit(solution)/shard_map/ppermute | solution.py:225
  40.6 0.6 %add_add_fusion.1 = f32[3,256]{1,0:T(4,128)} fusion(f32[3,256]{1,0:T(4,128)S(1)} %collective-permute-done.8, f32[3,256]{1,0:T(4,128)S(1)} %collective-permute-done.7, f32[3,256]{1,0:T(4,128)S(1)} %collective-permute-done.6, f32[3,1024]{1,0:T(4,128)S(1)} %add_add_fusion, s32[]{:T(128)S(6)} %select_n.12), kind=kLoop, calls=%fused_computation.2 | loop fusion | flops 2304 | bytes 15364 | tf_op jit(solution)/shard_map/add | solution.py:225
  (2 shorter events, 0.0 us)
Async XLA Ops:
  0.6 9.0 %copy-start.2 = (f32[16]{0:T(128)S(1)}, f32[16]{0:T(128)}, u32[]{:S(2)}) copy-start(f32[16]{0:T(128)} %table_ref.5) | copy-start | bytes 196
  0.6 9.0 %copy-start.3 = (s32[1,3]{1,0:T(1,128)S(1)}, s32[1,3]{1,0:T(1,128)}, u32[]{:S(2)}) copy-start(s32[1,3]{1,0:T(1,128)} %index_ref.5) | copy-start | bytes 40
  0.7 17.6 %collective-permute-start.1 = (bf16[1024,128]{1,0:T(8,128)(2,1)}, bf16[1024,128]{1,0:T(8,128)(2,1)S(1)}, u32[]{:S(2)}, u32[]{:S(2)}) collective-permute-start(bf16[1024,128]{1,0:T(8,128)(2,1)} %bitcast.3), channel_id=1, source_target_pairs={{0,4},{4,8},{8,12},{12,0},{1,5},{5,9},{9,13},{13,1},{2,6},{6,10},{... | collective-permute-start | bytes 786440 | tf_op jit(solution)/shard_map/ppermute | solution.py:22
  3.7 19.7 %collective-permute-start.3 = (bf16[1024,128]{1,0:T(8,128)(2,1)}, bf16[1024,128]{1,0:T(8,128)(2,1)S(1)}, u32[]{:S(2)}, u32[]{:S(2)}) collective-permute-start(bf16[1024,128]{1,0:T(8,128)(2,1)} %bitcast.4), channel_id=1, source_target_pairs={{0,12},{4,0},{8,4},{12,8},{1,13},{5,1},{9,5},{13,9},{2,14},{6,2},{... | collective-permute-start | bytes 786440 | tf_op jit(solution)/shard_map/ppermute | solution.py:22
  5.8 12.4 %collective-permute-start = (bf16[3,1024]{1,0:T(4,128)(2,1)}, bf16[3,1024]{1,0:T(4,128)(2,1)S(1)}, u32[]{:S(2)}, u32[]{:S(2)}) collective-permute-start(bf16[3,1024]{1,0:T(4,128)(2,1)} %rgeom_ref.3), channel_id=1, source_target_pairs={{0,4},{4,8},{8,12},{12,0},{1,5},{5,9},{9,13},{13,1},{2,6},{6,10},{... | collective-permute-start | bytes 18440 | tf_op jit(solution)/shard_map/ppermute | solution.py:22
  5.8 17.6 %collective-permute-start.2 = (bf16[3,1024]{1,0:T(4,128)(2,1)}, bf16[3,1024]{1,0:T(4,128)(2,1)S(1)}, u32[]{:S(2)}, u32[]{:S(2)}) collective-permute-start(bf16[3,1024]{1,0:T(4,128)(2,1)} %rgeom_ref.3), channel_id=1, source_target_pairs={{0,12},{4,0},{8,4},{12,8},{1,13},{5,1},{9,5},{13,9},{2,14},{6,2},{... | collective-permute-start | bytes 18440 | tf_op jit(solution)/shard_map/ppermute | solution.py:22
  9.6 1.0 %copy-start = (bf16[1,1024,128]{2,1,0:T(8,128)(2,1)S(1)}, bf16[1,1024,128]{2,1,0:T(8,128)(2,1)}, u32[]{:S(2)}) copy-start(bf16[1,1024,128]{2,1,0:T(8,128)(2,1)} %param.5) | copy-start | bytes 786436
  10.6 0.7 %copy-start.1 = (bf16[3,1024]{1,0:T(4,128)(2,1)S(1)}, bf16[3,1024]{1,0:T(4,128)(2,1)}, u32[]{:S(2)}) copy-start(bf16[3,1024]{1,0:T(4,128)(2,1)} %rgeom_ref.3) | copy-start | bytes 18436
  28.6 6.1 %collective-permute-start.4 = (f32[3,1024]{1,0:T(4,128)S(1)}, f32[3,1024]{1,0:T(4,128)S(1)}, u32[]{:S(2)}, u32[]{:S(2)}) collective-permute-start(f32[3,1024]{1,0:T(4,128)S(1)} %get-tuple-element.15), channel_id=1, source_target_pairs={{0,12},{4,0},{8,4},{12,8},{1,13},{5,1},{9,5},{13,9},{2,14},{6,2},{... | collective-permute-start | bytes 36872 | tf_op jit(solution)/shard_map/ppermute | solution.py:22
  30.4 5.5 %collective-permute-start.5 = (f32[3,1024]{1,0:T(4,128)S(1)}, f32[3,1024]{1,0:T(4,128)S(1)}, u32[]{:S(2)}, u32[]{:S(2)}) collective-permute-start(f32[3,1024]{1,0:T(4,128)S(1)} %get-tuple-element.16), channel_id=1, source_target_pairs={{0,4},{4,8},{8,12},{12,0},{1,5},{5,9},{9,13},{13,1},{2,6},{6,10},{... | collective-permute-start | bytes 36872 | tf_op jit(solution)/shard_map/ppermute | solution.py:22
  30.7 6.9 %collective-permute-start.10 = (f32[2,32,32]{2,1,0:T(8,128)S(1)}, f32[2,32,32]{2,1,0:T(8,128)S(1)}, u32[]{:S(2)}, u32[]{:S(2)}) collective-permute-start(f32[2,32,32]{2,1,0:T(8,128)S(1)} %get-tuple-element.17), channel_id=1, source_target_pairs={{0,4},{4,8},{8,12},{12,0},{1,5},{5,9},{9,13},{13,1},{2,6},{6,10},{... | collective-permute-start | bytes 24584 | tf_op jit(solution)/shard_map/ppermute | solution.py:22
  30.7 7.2 %collective-permute-start.11 = (f32[2,32,32]{2,1,0:T(8,128)S(1)}, f32[2,32,32]{2,1,0:T(8,128)S(1)}, u32[]{:S(2)}, u32[]{:S(2)}) collective-permute-start(f32[2,32,32]{2,1,0:T(8,128)S(1)} %get-tuple-element.17), channel_id=1, source_target_pairs={{0,8},{4,12},{8,0},{12,4},{1,9},{5,13},{9,1},{13,5},{2,10},{6,14},... | collective-permute-start | bytes 24584 | tf_op jit(solution)/shard_map/ppermute | solution.py:22
  34.8 3.9 %collective-permute-start.9 = (f32[2,32,32]{2,1,0:T(8,128)S(1)}, f32[2,32,32]{2,1,0:T(8,128)S(1)}, u32[]{:S(2)}, u32[]{:S(2)}) collective-permute-start(f32[2,32,32]{2,1,0:T(8,128)S(1)} %get-tuple-element.17), channel_id=1, source_target_pairs={{0,12},{4,0},{8,4},{12,8},{1,13},{5,1},{9,5},{13,9},{2,14},{6,2},{... | collective-permute-start | bytes 24584 | tf_op jit(solution)/shard_map/ppermute | solution.py:22
  35.9 3.4 %collective-permute-start.6 = (f32[3,256]{1,0:T(4,128)S(1)}, f32[3,256]{1,0:T(4,128)S(1)}, u32[]{:S(2)}, u32[]{:S(2)}) collective-permute-start(f32[3,256]{1,0:T(4,128)S(1)} %get-tuple-element.18), channel_id=1, source_target_pairs={{0,1},{1,0},{2,3},{3,2},{4,5},{5,4},{6,7},{7,6},{8,9},{9,8},{10,11... | collective-permute-start | bytes 9224 | tf_op jit(solution)/shard_map/ppermute | solution.py:225
  36.0 3.7 %collective-permute-start.7 = (f32[3,256]{1,0:T(4,128)S(1)}, f32[3,256]{1,0:T(4,128)S(1)}, u32[]{:S(2)}, u32[]{:S(2)}) collective-permute-start(f32[3,256]{1,0:T(4,128)S(1)} %get-tuple-element.20), channel_id=1, source_target_pairs={{0,2},{1,3},{2,0},{3,1},{4,6},{5,7},{6,4},{7,5},{8,10},{9,11},{10,... | collective-permute-start | bytes 9224 | tf_op jit(solution)/shard_map/ppermute | solution.py:225
  37.6 3.0 %collective-permute-start.8 = (f32[3,256]{1,0:T(4,128)S(1)}, f32[3,256]{1,0:T(4,128)S(1)}, u32[]{:S(2)}, u32[]{:S(2)}) collective-permute-start(f32[3,256]{1,0:T(4,128)S(1)} %get-tuple-element.19), channel_id=1, source_target_pairs={{0,3},{1,2},{2,1},{3,0},{4,7},{5,6},{6,5},{7,4},{8,11},{9,10},{10,... | collective-permute-start | bytes 9224 | tf_op jit(solution)/shard_map/ppermute | solution.py:225

commit v3 on v2

v3 whole, which is shorter than its diff:
```python
import functools
import math

import jax
import jax.numpy as jnp
from jax import lax
from jax.experimental import pallas as pl
from jax.experimental.pallas import tpu as pltpu
from jax.sharding import PartitionSpec as P

CHORD_SHIFT = 0.5
CORE_SQUARE = 0.25
CHUNK = 512

NN = (((1,), (0,)), ((), ()))
NT = (((1,), (1,)), ((), ()))


def passed_along(value, axis, steps):
    count = lax.axis_size(axis)
    pairs = [(source, (source + steps) % count) for source in range(count)]
    return lax.ppermute(value, axis, pairs)


def exchanged(value, axis, flip):
    pairs = [(source, source ^ flip) for source in range(lax.axis_size(axis))]
    return lax.ppermute(value, axis, pairs)


def product(left, right, dims, precision=None):
    return lax.dot_general(
        left, right, dims, preferred_element_type=jnp.float32, precision=precision
    )


def cosine_of(angle):
    turns = jnp.floor(angle * (0.5 / math.pi) + 0.5)
    half = 0.5 * ((angle - turns * 6.28125) - turns * (2.0 * math.pi - 6.28125))
    square = half * half
    value = 1.0 / math.factorial(12)
    for order in (10, 8, 6, 4, 2, 0):
        sign = -1.0 if order % 4 == 2 else 1.0
        value = value * square + sign / math.factorial(order)
    return 2.0 * value * value - 1.0


def turned_modes(flat, cosine, sine):
    cols = flat.shape[0] // 4
    real = [flat[:cols], flat[2 * cols : 3 * cols]]
    imag = [flat[cols : 2 * cols], flat[3 * cols :]]
    parts = []
    for re, im in zip(real, imag):
        parts += [re * cosine - im * sine, re * sine + im * cosine]
    return jnp.concatenate(parts, axis=0)


def crosswise(value):
    cols = value.shape[0] // 4
    p, q, r, s = (value[k * cols : (k + 1) * cols] for k in range(4))
    return jnp.concatenate([-s, r, -q, p], axis=0)


def halves(value):
    high = value.astype(jnp.bfloat16)
    low = (value - high.astype(jnp.float32)).astype(jnp.bfloat16)
    return high, low


def moment_rows(pos):
    count = pos.shape[1]
    return jnp.concatenate(
        [jnp.ones((1, count), jnp.float32), pos, jnp.zeros((12, count), jnp.float32)], axis=0
    ).astype(jnp.bfloat16)


def tile_kernel(
    offset, plan, table_ref, index_ref, rgeom_ref, rmodes_ref, sgeom_ref, smodes_ref, *refs
):
    held = refs[: plan.held]
    grads = refs[plan.held : plan.held + plan.grads]
    force_ref, back_ref, backm_ref, row_ref, *rest = refs[plan.held + plan.grads :]
    if plan.role == "own":
        geom_buf, modes_buf, sems = rest
        copies = [
            pltpu.make_async_copy(rgeom_ref, geom_buf, sems.at[0]),
            pltpu.make_async_copy(rmodes_ref, modes_buf, sems.at[1]),
        ]
        for copy in copies:
            copy.start()
        for copy in copies:
            copy.wait()
        rgeom_ref, rmodes_ref = geom_buf, modes_buf
    count, full = rmodes_ref.shape
    cols = full // 4
    wave = table_ref[index_ref[0, offset]]
    rpos = rgeom_ref[...].astype(jnp.float32)
    rflat = rmodes_ref[...].astype(jnp.float32).T
    if plan.role == "own":
        spos, sflat = rpos, rflat
    else:
        spos = sgeom_ref[...].astype(jnp.float32)
        sflat = smodes_ref[...].astype(jnp.float32).T
    rangle = wave * (rpos[0:1] + CHORD_SHIFT)
    sangle = wave * spos[0:1]
    quarter_turn = 0.5 * math.pi
    circle = cosine_of(
        jnp.concatenate([rangle, rangle - quarter_turn, sangle, sangle - quarter_turn], axis=0)
    )
    recv = turned_modes(rflat, circle[0:1], circle[1:2])
    send = turned_modes(sflat, circle[2:3], circle[3:4])
    rhigh, rlow = halves(recv)
    shigh, slow = halves(send)
    rboth = jnp.concatenate([rhigh, rlow[: 2 * cols]], axis=0)
    rows = jnp.concatenate([crosswise(rhigh), crosswise(rlow)], axis=0).T
    cross = crosswise(jnp.concatenate([shigh[2 * cols :], shigh[: 2 * cols]], axis=0))
    paired = jnp.concatenate([cross, cross], axis=0)
    srows = jnp.concatenate([shigh, slow[2 * cols :], slow[2 * cols :]], axis=0).T
    rmom = moment_rows(rpos)
    smom = moment_rows(spos)
    smom_rows = jnp.concatenate(
        [smom.astype(jnp.float32), jnp.zeros((full - 16, count), jnp.float32)], axis=0
    ).T.astype(jnp.bfloat16)
    place = jnp.concatenate([rpos, jnp.zeros((5, count), jnp.float32)], axis=0).T
    lane = lax.broadcasted_iota(jnp.int32, (CHUNK, full), 1)
    def stage_l(start):
        return product(rows[start:start+CHUNK], paired, NN)

    def stage_v(start, along):
        part = slice(start, start + CHUNK)
        dx = (place[part, 0:1] + CHORD_SHIFT) - spos[0:1]
        dy = place[part, 1:2] - spos[1:2]
        dz = place[part, 2:3] - spos[2:3]
        inverse = lax.rsqrt(dx * dx + dy * dy + (dz * dz + CORE_SQUARE))
        kernel = inverse.astype(jnp.bfloat16)
        cubed = ((inverse * inverse) * (inverse * along)).astype(jnp.bfloat16)
        return kernel, cubed

    def stage_m(start, kernel, cubed):
        part = slice(start, start + CHUNK)
        ahead = product(kernel, srows[:, :full], NN)
        moments = product(cubed, smom_rows, NN)
        back = product(rboth[:, part], kernel, NN)
        backm = product(rmom[:, part], cubed, NN)
        both = rows[part].astype(jnp.float32)
        turn = jnp.sum((both[:, :full] + both[:, full:]) * ahead, axis=1, keepdims=True)
        row_ref[:, part] = jnp.where(lane == 4, turn, moments).T[:8]
        return back, backm

    starts = list(range(0, count, CHUNK))
    along = stage_l(0)
    pair = stage_v(0, along)
    for k, start in enumerate(starts):
        nxt = None
        if k + 1 < len(starts):
            along = stage_l(starts[k + 1])
        back, backm = stage_m(start, *pair)
        if k + 1 < len(starts):
            pair = stage_v(starts[k + 1], along)
        if k == 0:
            back_ref[...] = back
            backm_ref[...] = backm
        else:
            back_ref[...] += back
            backm_ref[...] += backm
    behind = back_ref[: full] + jnp.concatenate(
        [back_ref[full:], jnp.zeros((2 * cols, count), jnp.float32)], axis=0
    )

    def quarter(value, k):
        return value[k * cols : (k + 1) * cols]

    col_turn = wave * jnp.sum(
        quarter(behind, 0) * quarter(send, 3)
        - quarter(behind, 1) * quarter(send, 2)
        + quarter(behind, 2) * quarter(send, 1)
        - quarter(behind, 3) * quarter(send, 0),
        axis=0,
        keepdims=True,
    )
    rm = row_ref[...]
    sm = backm_ref[...]
    row = jnp.concatenate(
        [
            wave * rm[4:5] - ((rpos[0:1] + CHORD_SHIFT) * rm[0:1] - rm[1:2]),
            rm[2:3] - rpos[1:2] * rm[0:1],
            rm[3:4] - rpos[2:3] * rm[0:1],
        ],
        axis=0,
    ) * plan.grad_scale
    col = jnp.concatenate(
        [
            (sm[1:2] + CHORD_SHIFT * sm[0:1] - spos[0:1] * sm[0:1]) - col_turn,
            sm[2:3] - spos[1:2] * sm[0:1],
            sm[3:4] - spos[2:3] * sm[0:1],
        ],
        axis=0,
    ) * plan.grad_scale
    bhigh, blow = halves(behind[: 2 * cols])
    gram = product(jnp.concatenate([bhigh, blow], axis=0), srows, NN)
    gram = (
        gram[: 2 * cols, 2 * cols : full]
        + gram[2 * cols :, 2 * cols : full]
        + gram[: 2 * cols, full : full + 2 * cols]
    )
    force_real = (gram[:cols, :cols] + gram[cols:, cols:]) * plan.force_scale
    force_imag = (gram[:cols, cols:] - gram[cols:, :cols]) * plan.force_scale
    if plan.role == "own":
        grads[0][...] = row + col
        force_ref[0] = force_real
        force_ref[1] = force_imag
    else:
        grads[0][...] = held[0][...] + row
        grads[1][...] = col
        force_ref[0] = held[1][0] + force_real
        force_ref[1] = held[1][1] + force_imag


class Plan:
    def __init__(self, role, grad_scale, force_scale):
        self.role = role
        self.grad_scale = grad_scale
        self.force_scale = force_scale
        self.held = 0 if role == "own" else 2
        self.grads = 1 if role == "own" else 2


def tile_terms(offset, plan, table, index, recv, send, *held):
    count, width = recv[1].shape
    cols = width // 4
    smem = pl.BlockSpec(memory_space=pltpu.SMEM)
    vmem = pl.BlockSpec(memory_space=pltpu.VMEM)
    grad = jax.ShapeDtypeStruct((3, count), jnp.float32)
    force = jax.ShapeDtypeStruct((2, cols, cols), jnp.float32)
    operands = [vmem] * 4
    extra = []
    if plan.role == "own":
        operands = [pl.BlockSpec(memory_space=pl.ANY)] * 4
        extra = [
            pltpu.VMEM(recv[0].shape, recv[0].dtype),
            pltpu.VMEM(recv[1].shape, recv[1].dtype),
            pltpu.SemaphoreType.DMA((2,)),
        ]
    return pl.pallas_call(
        functools.partial(tile_kernel, offset, plan),
        out_shape=(grad,) * plan.grads + (force,),
        in_specs=[smem, smem] + operands + [vmem] * plan.held,
        out_specs=(vmem,) * (plan.grads + 1),
        scratch_shapes=[
            pltpu.VMEM((width + 2 * cols, count), jnp.float32),
            pltpu.VMEM((16, count), jnp.float32),
            pltpu.VMEM((8, count), jnp.float32),
        ]
        + extra,
        name="tile_%d" % offset,
        compiler_params=pltpu.CompilerParams(vmem_limit_bytes=48 << 20),
        cost_estimate=pl.CostEstimate(
            flops=2 * count * count * width * 6,
            transcendentals=count * count,
            bytes_accessed=4 * count * width,
        ),
    )(table, index, *recv, *send, *held)


def local(geometry, modes, reduced_freq, freq_index):
    row_count = geometry.shape[1]
    own = (geometry, modes[0])
    columns = modes.shape[2] // 4
    steps = freq_index.shape[1]
    blocks = lax.axis_size("blk")
    freqs = lax.axis_size("freq")
    grad_scale = 1.0 / math.sqrt(columns * steps * row_count * freqs)
    force_scale = 1.0 / math.sqrt(row_count * row_count * blocks * steps)

    def terms(offset, *operands):
        plan = Plan("sent" if offset else "own", grad_scale, force_scale)
        return tile_terms(offset, plan, reduced_freq, freq_index, *operands)

    sender = passed_along(own, "blk", 1)
    mine, force = terms(0, own, own)
    sender, mine = lax.optimization_barrier((sender, mine))
    returned = []
    for offset in range(1, steps):
        current = sender
        if offset + 1 < steps:
            sender = passed_along(current, "blk", 1)
        mine, back, force = terms(offset, own, current, mine, force)
        returned.append(passed_along(back, "blk", -offset))
    total = mine
    for back in returned:
        total = total + back
    if blocks == 4:
        pair = force + passed_along(force, "blk", -2)
        force_total = pair + exchanged(pair, "blk", 1)
    else:
        force_total = lax.psum(force, "blk")
    share = row_count // freqs
    place = lax.axis_index("freq")
    result = lax.dynamic_slice_in_dim(total, place * share, share, axis=1)
    for flip in range(1, freqs):
        piece = lax.dynamic_slice_in_dim(total, (place ^ flip) * share, share, axis=1)
        result = result + exchanged(piece, "freq", flip)
    return (result, force_total[None])


def solution(mesh):
    return jax.shard_map(
        local,
        mesh=mesh,
        in_specs=(
            P(None, ("case", "blk")),
            P("freq", ("case", "blk"), None),
            P(),
            P(("case", "freq"), None),
        ),
        out_specs=(P(None, ("case", "blk", "freq")), P(("case", "freq"), None, None, None)),
        check_vma=False,
    )
```

time: 41.4 us -> 38.2 us (0.923)
  starting transfers between devices: 17 us -> 14.3 us
  Pallas kernels: 15.5 us -> 13.7 us
  waiting for transfers between devices: 5.02 us -> 6.33 us
    ppermute x9 -> x7, starting transfers between devices: 15.1 us -> 12.3 us  [passed_along(): return lax.ppermute(value, axis, pairs)]
    ppermute x3 -> x4, waiting for transfers between devices: 1.31 us -> 3.29 us  [exchanged(): return lax.ppermute(value, axis, pairs)]
    pallas_call x3, Pallas kernels: 15.5 us -> 13.7 us  [tile_terms(): pl.pallas_call(functools.partial(tile_kernel, offset, plan), out_shape=(g...]
    ppermute x9 -> x7, waiting for transfers between devices: 3.71 us -> 3.03 us  [passed_along(): return lax.ppermute(value, axis, pairs)]
    ppermute x3 -> x4, starting transfers between devices: 1.93 us -> 2 us  [exchanged(): return lax.ppermute(value, axis, pairs)]
  transfers between devices with their start and end apart: 12 -> 11, of which waited for: 5 -> 6; matrix products, arithmetic and copies ran while one was open for 2% -> 2% of each run, Pallas kernels for 25% -> 36%
where the time goes in v3:
time: 38.2 us; the launch traced here: 38 us
  starting transfers between devices  14.3 us (37%)
  Pallas kernels  13.7 us (36%)
  waiting for transfers between devices  6.33 us (17%)
  local copies, waits for them, and re-layouts  1.67 us (4%)
  other arithmetic  1.23 us (3%)
  between operations  0.75 us (2%)
    pallas_call x3, Pallas kernels, tile_terms(): pl.pallas_call(functools.partial(tile_kernel, offset, plan), out_shape=(g...  13.7 us
    ppermute x7, starting transfers between devices, passed_along(): return lax.ppermute(value, axis, pairs)  12.3 us
    ppermute x4, waiting for transfers between devices, exchanged(): return lax.ppermute(value, axis, pairs)  3.29 us
    ppermute x7, waiting for transfers between devices, passed_along(): return lax.ppermute(value, axis, pairs)  3.03 us
    ppermute x4, starting transfers between devices, exchanged(): return lax.ppermute(value, axis, pairs)  2 us
    unnamed x8, local copies, waits for them, and re-layouts  1.66 us
  transfers between devices with their start and end apart: 11, of which 6 were waited for; matrix products, arithmetic and copies ran while one was open for 2% of the time, Pallas kernels for 36%

profile of v3, /device:TPU:0, one launch (start us, length us, event | category | flops | bytes accessed | tf_op | source)
XLA Modules:
  0.0 38.0 jit_solution(2551364820278673350)
XLA Ops:
  0.6 0.0 copy-start.2
  0.6 0.0 copy-start.3
  0.7 3.1 %collective-permute-start.1 = (bf16[1024,128]{1,0:T(8,128)(2,1)}, bf16[1024,128]{1,0:T(8,128)(2,1)S(1)}, u32[]{:S(2)}, u32[]{:S(2)}) collective-permute-start(bf16[1024,128]{1,0:T(8,128)(2,1)} %bitcast.3), channel_id=1, source_target_pairs={{0,4},{4,8},{8,12},{12,0},{1,5},{5,9},{9,13},{13,1},{2,6},{6,10},{... | collective-permute-start | bytes 786440 | tf_op jit(solution)/shard_map/ppermute | solution.py:22
  3.7 1.6 %collective-permute-start = (bf16[3,1024]{1,0:T(4,128)(2,1)}, bf16[3,1024]{1,0:T(4,128)(2,1)S(1)}, u32[]{:S(2)}, u32[]{:S(2)}) collective-permute-start(bf16[3,1024]{1,0:T(4,128)(2,1)} %rgeom_ref.5), channel_id=1, source_target_pairs={{0,4},{4,8},{8,12},{12,0},{1,5},{5,9},{9,13},{13,1},{2,6},{6,10},{... | collective-permute-start | bytes 18440 | tf_op jit(solution)/shard_map/ppermute | solution.py:22
  5.3 0.0 copy-done.2
  5.3 0.0 copy-done.3
  5.3 0.0 copy-start
  5.3 0.9 %copy-done = bf16[1,1024,128]{2,1,0:T(8,128)(2,1)S(1)} copy-done((bf16[1,1024,128]{2,1,0:T(8,128)(2,1)S(1)}, bf16[1,1024,128]{2,1,0:T(8,128)(2,1)}, u32[]{:S(2)}) %copy-start) | copy-done | bytes 262168
  6.3 0.0 copy-start.1
  6.3 0.7 %copy-done.1 = bf16[3,1024]{1,0:T(4,128)(2,1)S(1)} copy-done((bf16[3,1024]{1,0:T(4,128)(2,1)S(1)}, bf16[3,1024]{1,0:T(4,128)(2,1)}, u32[]{:S(2)}) %copy-start.1) | copy-done | bytes 6168
  7.0 4.5 %tile_0.1 = (f32[3,1024]{1,0:T(4,128)S(1)}, f32[2,32,32]{2,1,0:T(8,128)S(1)}) custom-call(f32[16]{0:T(128)S(1)} %copy-done.2, s32[1,3]{1,0:T(1,128)S(1)} %copy-done.3, bf16[3,1024]{1,0:T(4,128)(2,1)S(1)} %copy-done.1, bf16[1024,128]{1,0:T(8,128)(2,1)S(1)} %bitcast.4, bf16[3,1024]{1,0:T(4,128)(2,1)S(1)} %copy-done.1, bf16[1024,128]{1,0:T(8,128)(2,1)S(1)} %bitcast.5), custom_call_target="tpu_custom_call" | custom-call | flops 1610612736 | bytes 524288 | tf_op jit(solution)/shard_map/tile_0/pallas_call | solution.py:243
  11.4 1.0 %collective-permute-done.sgeom_ref = bf16[3,1024]{1,0:T(4,128)(2,1)S(1)} collective-permute-done((bf16[3,1024]{1,0:T(4,128)(2,1)}, bf16[3,1024]{1,0:T(4,128)(2,1)S(1)}, u32[]{:S(2)}, u32[]{:S(2)}) %collective-permute-start) | collective-permute-done | bytes 6176 | tf_op jit(solution)/shard_map/ppermute | solution.py:22
  12.4 0.0 collective-permute-done.1.smodes_ref
  12.4 0.6 %collective-permute-start.3 = (bf16[1024,128]{1,0:T(8,128)(2,1)S(1)}, bf16[1024,128]{1,0:T(8,128)(2,1)S(1)}, u32[]{:S(2)}, u32[]{:S(2)}) collective-permute-start(bf16[1024,128]{1,0:T(8,128)(2,1)S(1)} %collective-permute-done.1.smodes_ref), channel_id=1, source_target_pairs={{0,4},{4,8},{8,12},{12,0},{1,5},{5,9},{9,13},{13,1},{2,6},{6,10},{... | collective-permute-start | bytes 786440 | tf_op jit(solution)/shard_map/ppermute | solution.py:22
  13.1 0.7 %collective-permute-start.2 = (bf16[3,1024]{1,0:T(4,128)(2,1)S(1)}, bf16[3,1024]{1,0:T(4,128)(2,1)S(1)}, u32[]{:S(2)}, u32[]{:S(2)}) collective-permute-start(bf16[3,1024]{1,0:T(4,128)(2,1)S(1)} %collective-permute-done.sgeom_ref), channel_id=1, source_target_pairs={{0,4},{4,8},{8,12},{12,0},{1,5},{5,9},{9,13},{13,1},{2,6},{6,10},{... | collective-permute-start | bytes 18440 | tf_op jit(solution)/shard_map/ppermute | solution.py:22
  13.7 4.6 %tile_1.1 = (f32[3,1024]{1,0:T(4,128)S(1)}, f32[3,1024]{1,0:T(4,128)S(1)}, f32[2,32,32]{2,1,0:T(8,128)S(1)}) custom-call(f32[16]{0:T(128)S(1)} %copy-done.2, s32[1,3]{1,0:T(1,128)S(1)} %copy-done.3, bf16[3,1024]{1,0:T(4,128)(2,1)S(1)} %copy-done.1, bf16[1024,128]{1,0:T(8,128)(2,1)S(1)} %bitcast.6, bf16[3,1024]{1,0:T(4,128)(2,1)S(1)} %collective-permute-done.sgeom_ref, ...), custom_call_target="tpu_custom_call" | custom-call | flops 1610612736 | bytes 524288 | tf_op jit(solution)/shard_map/tile_1/pallas_call | solution.py:243
  18.4 3.4 %collective-permute-start.4 = (f32[3,1024]{1,0:T(4,128)S(1)}, f32[3,1024]{1,0:T(4,128)S(1)}, u32[]{:S(2)}, u32[]{:S(2)}) collective-permute-start(f32[3,1024]{1,0:T(4,128)S(1)} %get-tuple-element.21), channel_id=1, source_target_pairs={{0,12},{4,0},{8,4},{12,8},{1,13},{5,1},{9,5},{13,9},{2,14},{6,2},{... | collective-permute-start | bytes 36872 | tf_op jit(solution)/shard_map/ppermute | solution.py:22
  21.8 0.3 collective-permute-done.2.sgeom_ref
  22.1 0.0 collective-permute-done.3.smodes_ref
  22.1 4.6 %tile_2.1 = (f32[3,1024]{1,0:T(4,128)S(1)}, f32[3,1024]{1,0:T(4,128)S(1)}, f32[2,32,32]{2,1,0:T(8,128)S(1)}) custom-call(f32[16]{0:T(128)S(1)} %copy-done.2, s32[1,3]{1,0:T(1,128)S(1)} %copy-done.3, bf16[3,1024]{1,0:T(4,128)(2,1)S(1)} %copy-done.1, bf16[1024,128]{1,0:T(8,128)(2,1)S(1)} %bitcast.7, bf16[3,1024]{1,0:T(4,128)(2,1)S(1)} %collective-permute-done.2.sgeom_ref, ...), custom_call_target="tpu_custom_call" | custom-call | flops 1610612736 | bytes 524288 | tf_op jit(solution)/shard_map/tile_2/pallas_call | solution.py:243
  26.7 0.1 collective-permute-start.5
  26.8 2.9 %collective-permute-start.9 = (f32[2,32,32]{2,1,0:T(8,128)S(1)}, f32[2,32,32]{2,1,0:T(8,128)S(1)}, u32[]{:S(2)}, u32[]{:S(2)}) collective-permute-start(f32[2,32,32]{2,1,0:T(8,128)S(1)} %get-tuple-element.23), channel_id=1, source_target_pairs={{0,8},{4,12},{8,0},{12,4},{1,9},{5,13},{9,1},{13,5},{2,10},{6,14},... | collective-permute-start | bytes 24584 | tf_op jit(solution)/shard_map/ppermute | solution.py:22
  29.7 0.0 collective-permute-done.4
  29.7 1.7 %collective-permute-done.5 = f32[3,1024]{1,0:T(4,128)S(1)} collective-permute-done((f32[3,1024]{1,0:T(4,128)S(1)}, f32[3,1024]{1,0:T(4,128)S(1)}, u32[]{:S(2)}, u32[]{:S(2)}) %collective-permute-start.5) | collective-permute-done | bytes 12320 | tf_op jit(solution)/shard_map/ppermute | solution.py:22
  31.5 0.1 collective-permute-start.6
  31.5 1.3 %collective-permute-start.7 = (f32[3,256]{1,0:T(4,128)S(1)}, f32[3,256]{1,0:T(4,128)S(1)}, u32[]{:S(2)}, u32[]{:S(2)}) collective-permute-start(f32[3,256]{1,0:T(4,128)S(1)} %get-tuple-element.26), channel_id=1, source_target_pairs={{0,2},{1,3},{2,0},{3,1},{4,6},{5,7},{6,4},{7,5},{8,10},{9,11},{10,... | collective-permute-start | bytes 9224 | tf_op jit(solution)/shard_map/ppermute | solution.py:27
  32.8 0.6 %collective-permute-start.8 = (f32[3,256]{1,0:T(4,128)S(1)}, f32[3,256]{1,0:T(4,128)S(1)}, u32[]{:S(2)}, u32[]{:S(2)}) collective-permute-start(f32[3,256]{1,0:T(4,128)S(1)} %get-tuple-element.25), channel_id=1, source_target_pairs={{0,3},{1,2},{2,1},{3,0},{4,7},{5,6},{6,5},{7,4},{8,11},{9,10},{10,... | collective-permute-start | bytes 9224 | tf_op jit(solution)/shard_map/ppermute | solution.py:27
  33.4 0.0 collective-permute-done.9
  33.4 0.1 collective-permute-start.10
  33.5 0.0 collective-permute-done.6
  33.5 1.7 %collective-permute-done.7 = f32[3,256]{1,0:T(4,128)S(1)} collective-permute-done((f32[3,256]{1,0:T(4,128)S(1)}, f32[3,256]{1,0:T(4,128)S(1)}, u32[]{:S(2)}, u32[]{:S(2)}) %collective-permute-start.7) | collective-permute-done | bytes 3104 | tf_op jit(solution)/shard_map/ppermute | solution.py:27
  35.2 0.6 %collective-permute-done.8 = f32[3,256]{1,0:T(4,128)S(1)} collective-permute-done((f32[3,256]{1,0:T(4,128)S(1)}, f32[3,256]{1,0:T(4,128)S(1)}, u32[]{:S(2)}, u32[]{:S(2)}) %collective-permute-start.8) | collective-permute-done | bytes 3104 | tf_op jit(solution)/shard_map/ppermute | solution.py:27
  35.8 0.6 %add_add_fusion.1 = f32[3,256]{1,0:T(4,128)} fusion(f32[3,256]{1,0:T(4,128)S(1)} %collective-permute-done.8, f32[3,256]{1,0:T(4,128)S(1)} %collective-permute-done.7, f32[3,256]{1,0:T(4,128)S(1)} %collective-permute-done.6, f32[3,1024]{1,0:T(4,128)S(1)} %add_add_fusion, s32[]{:T(128)S(6)} %select_n.12), kind=kLoop, calls=%fused_computation.2 | loop fusion | flops 2304 | bytes 15364 | tf_op jit(solution)/shard_map/add | solution.py:301
  36.4 1.0 %collective-permute-done.10 = f32[2,32,32]{2,1,0:T(8,128)S(1)} collective-permute-done((f32[2,32,32]{2,1,0:T(8,128)S(1)}, f32[2,32,32]{2,1,0:T(8,128)S(1)}, u32[]{:S(2)}, u32[]{:S(2)}) %collective-permute-start.10) | collective-permute-done | bytes 8224 | tf_op jit(solution)/shard_map/ppermute | solution.py:27
  37.4 0.6 %add_bitcast_fusion = f32[1,2,32,32]{3,2,1,0:T(8,128)} fusion(f32[2,32,32]{2,1,0:T(8,128)S(1)} %add.42, f32[2,32,32]{2,1,0:T(8,128)S(1)} %collective-permute-done.10), kind=kLoop, calls=%fused_computation | loop fusion | flops 2048 | bytes 24576 | tf_op jit(solution)/shard_map/broadcast_in_dim | solution.py:302
  (3 shorter events, 0.0 us)
Async XLA Ops:
  0.6 4.7 %copy-start.2 = (f32[16]{0:T(128)S(1)}, f32[16]{0:T(128)}, u32[]{:S(2)}) copy-start(f32[16]{0:T(128)} %table_ref.5) | copy-start | bytes 196
  0.6 4.7 %copy-start.3 = (s32[1,3]{1,0:T(1,128)S(1)}, s32[1,3]{1,0:T(1,128)}, u32[]{:S(2)}) copy-start(s32[1,3]{1,0:T(1,128)} %index_ref.5) | copy-start | bytes 40
  0.7 11.8 %collective-permute-start.1 = (bf16[1024,128]{1,0:T(8,128)(2,1)}, bf16[1024,128]{1,0:T(8,128)(2,1)S(1)}, u32[]{:S(2)}, u32[]{:S(2)}) collective-permute-start(bf16[1024,128]{1,0:T(8,128)(2,1)} %bitcast.3), channel_id=1, source_target_pairs={{0,4},{4,8},{8,12},{12,0},{1,5},{5,9},{9,13},{13,1},{2,6},{6,10},{... | collective-permute-start | bytes 786440 | tf_op jit(solution)/shard_map/ppermute | solution.py:22
  3.7 8.7 %collective-permute-start = (bf16[3,1024]{1,0:T(4,128)(2,1)}, bf16[3,1024]{1,0:T(4,128)(2,1)S(1)}, u32[]{:S(2)}, u32[]{:S(2)}) collective-permute-start(bf16[3,1024]{1,0:T(4,128)(2,1)} %rgeom_ref.5), channel_id=1, source_target_pairs={{0,4},{4,8},{8,12},{12,0},{1,5},{5,9},{9,13},{13,1},{2,6},{6,10},{... | collective-permute-start | bytes 18440 | tf_op jit(solution)/shard_map/ppermute | solution.py:22
  5.3 1.0 %copy-start = (bf16[1,1024,128]{2,1,0:T(8,128)(2,1)S(1)}, bf16[1,1024,128]{2,1,0:T(8,128)(2,1)}, u32[]{:S(2)}) copy-start(bf16[1,1024,128]{2,1,0:T(8,128)(2,1)} %param.5) | copy-start | bytes 786436
  6.3 0.7 %copy-start.1 = (bf16[3,1024]{1,0:T(4,128)(2,1)S(1)}, bf16[3,1024]{1,0:T(4,128)(2,1)}, u32[]{:S(2)}) copy-start(bf16[3,1024]{1,0:T(4,128)(2,1)} %rgeom_ref.5) | copy-start | bytes 18436
  12.4 9.6 %collective-permute-start.3 = (bf16[1024,128]{1,0:T(8,128)(2,1)S(1)}, bf16[1024,128]{1,0:T(8,128)(2,1)S(1)}, u32[]{:S(2)}, u32[]{:S(2)}) collective-permute-start(bf16[1024,128]{1,0:T(8,128)(2,1)S(1)} %collective-permute-done.1.smodes_ref), channel_id=1, source_target_pairs={{0,4},{4,8},{8,12},{12,0},{1,5},{5,9},{9,13},{13,1},{2,6},{6,10},{... | collective-permute-start | bytes 786440 | tf_op jit(solution)/shard_map/ppermute | solution.py:22
  13.1 9.0 %collective-permute-start.2 = (bf16[3,1024]{1,0:T(4,128)(2,1)S(1)}, bf16[3,1024]{1,0:T(4,128)(2,1)S(1)}, u32[]{:S(2)}, u32[]{:S(2)}) collective-permute-start(bf16[3,1024]{1,0:T(4,128)(2,1)S(1)} %collective-permute-done.sgeom_ref), channel_id=1, source_target_pairs={{0,4},{4,8},{8,12},{12,0},{1,5},{5,9},{9,13},{13,1},{2,6},{6,10},{... | collective-permute-start | bytes 18440 | tf_op jit(solution)/shard_map/ppermute | solution.py:22
  18.4 11.3 %collective-permute-start.4 = (f32[3,1024]{1,0:T(4,128)S(1)}, f32[3,1024]{1,0:T(4,128)S(1)}, u32[]{:S(2)}, u32[]{:S(2)}) collective-permute-start(f32[3,1024]{1,0:T(4,128)S(1)} %get-tuple-element.21), channel_id=1, source_target_pairs={{0,12},{4,0},{8,4},{12,8},{1,13},{5,1},{9,5},{13,9},{2,14},{6,2},{... | collective-permute-start | bytes 36872 | tf_op jit(solution)/shard_map/ppermute | solution.py:22
  26.7 4.7 %collective-permute-start.5 = (f32[3,1024]{1,0:T(4,128)S(1)}, f32[3,1024]{1,0:T(4,128)S(1)}, u32[]{:S(2)}, u32[]{:S(2)}) collective-permute-start(f32[3,1024]{1,0:T(4,128)S(1)} %get-tuple-element.22), channel_id=1, source_target_pairs={{0,8},{4,12},{8,0},{12,4},{1,9},{5,13},{9,1},{13,5},{2,10},{6,14},... | collective-permute-start | bytes 36872 | tf_op jit(solution)/shard_map/ppermute | solution.py:22
  26.8 6.6 %collective-permute-start.9 = (f32[2,32,32]{2,1,0:T(8,128)S(1)}, f32[2,32,32]{2,1,0:T(8,128)S(1)}, u32[]{:S(2)}, u32[]{:S(2)}) collective-permute-start(f32[2,32,32]{2,1,0:T(8,128)S(1)} %get-tuple-element.23), channel_id=1, source_target_pairs={{0,8},{4,12},{8,0},{12,4},{1,9},{5,13},{9,1},{13,5},{2,10},{6,14},... | collective-permute-start | bytes 24584 | tf_op jit(solution)/shard_map/ppermute | solution.py:22
  31.5 2.0 %collective-permute-start.6 = (f32[3,256]{1,0:T(4,128)S(1)}, f32[3,256]{1,0:T(4,128)S(1)}, u32[]{:S(2)}, u32[]{:S(2)}) collective-permute-start(f32[3,256]{1,0:T(4,128)S(1)} %get-tuple-element.24), channel_id=1, source_target_pairs={{0,1},{1,0},{2,3},{3,2},{4,5},{5,4},{6,7},{7,6},{8,9},{9,8},{10,11... | collective-permute-start | bytes 9224 | tf_op jit(solution)/shard_map/ppermute | solution.py:27
  31.5 3.7 %collective-permute-start.7 = (f32[3,256]{1,0:T(4,128)S(1)}, f32[3,256]{1,0:T(4,128)S(1)}, u32[]{:S(2)}, u32[]{:S(2)}) collective-permute-start(f32[3,256]{1,0:T(4,128)S(1)} %get-tuple-element.26), channel_id=1, source_target_pairs={{0,2},{1,3},{2,0},{3,1},{4,6},{5,7},{6,4},{7,5},{8,10},{9,11},{10,... | collective-permute-start | bytes 9224 | tf_op jit(solution)/shard_map/ppermute | solution.py:27
  32.8 3.0 %collective-permute-start.8 = (f32[3,256]{1,0:T(4,128)S(1)}, f32[3,256]{1,0:T(4,128)S(1)}, u32[]{:S(2)}, u32[]{:S(2)}) collective-permute-start(f32[3,256]{1,0:T(4,128)S(1)} %get-tuple-element.25), channel_id=1, source_target_pairs={{0,3},{1,2},{2,1},{3,0},{4,7},{5,6},{6,5},{7,4},{8,11},{9,10},{10,... | collective-permute-start | bytes 9224 | tf_op jit(solution)/shard_map/ppermute | solution.py:27
  33.4 4.0 %collective-permute-start.10 = (f32[2,32,32]{2,1,0:T(8,128)S(1)}, f32[2,32,32]{2,1,0:T(8,128)S(1)}, u32[]{:S(2)}, u32[]{:S(2)}) collective-permute-start(f32[2,32,32]{2,1,0:T(8,128)S(1)} %add.42), channel_id=1, source_target_pairs={{0,4},{4,0},{8,12},{12,8},{1,5},{5,1},{9,13},{13,9},{2,6},{6,2},{1... | collective-permute-start | bytes 24584 | tf_op jit(solution)/shard_map/ppermute | solution.py:27

commit v4 on v3

--- a/solution.py
+++ b/solution.py
@@ -73,45 +73,91 @@
     ).astype(jnp.bfloat16)
 
 
-def tile_kernel(
-    offset, plan, table_ref, index_ref, rgeom_ref, rmodes_ref, sgeom_ref, smodes_ref, *refs
-):
-    held = refs[: plan.held]
-    grads = refs[plan.held : plan.held + plan.grads]
-    force_ref, back_ref, backm_ref, row_ref, *rest = refs[plan.held + plan.grads :]
-    if plan.role == "own":
-        geom_buf, modes_buf, sems = rest
+def tile_kernel(offset, plan, *refs):
+    refs = list(refs)
+
+    def taken(number):
+        return [refs.pop(0) for _ in range(number)]
+
+    if plan.role == "own":
+        table_ref, index_ref, rgeom_ref, rmodes_ref = taken(4)
+    else:
+        waves_ref, rgeom_ref, rmodes_ref, sgeom_ref, smodes_ref = taken(5)
+    if plan.emits:
+        (next_ref,) = taken(1)
+    if plan.ready:
+        near_ref, cube_ref, rows_ref, rboth_ref = taken(4)
+    held = taken(plan.held)
+    grads = taken(plan.grads)
+    if not plan.last:
+        (force_ref,) = taken(1)
+    if plan.role == "own":
+        waves_out, geom_out, modes_out = taken(3)
+    if plan.emits:
+        near_out, cube_out, rows_out, rboth_out = taken(4)
+    back_ref, backm_ref, row_ref = taken(3)
+    if plan.role == "own":
+        table_buf, index_buf, sems = taken(3)
         copies = [
-            pltpu.make_async_copy(rgeom_ref, geom_buf, sems.at[0]),
-            pltpu.make_async_copy(rmodes_ref, modes_buf, sems.at[1]),
+            pltpu.make_async_copy(rgeom_ref, geom_out, sems.at[0]),
+            pltpu.make_async_copy(rmodes_ref, modes_out, sems.at[1]),
+            pltpu.make_async_copy(table_ref, table_buf, sems.at[2]),
+            pltpu.make_async_copy(index_ref, index_buf, sems.at[3]),
         ]
         for copy in copies:
             copy.start()
         for copy in copies:
             copy.wait()
-        rgeom_ref, rmodes_ref = geom_buf, modes_buf
+        rgeom_ref, rmodes_ref = geom_out, modes_out
+        wave = table_buf[index_buf[0, offset]]
+        for step in range(index_buf.shape[1]):
+            value = table_buf[index_buf[0, step]]
+            waves_out[step : step + 1] = jnp.full((1, waves_out.shape[1]), value, jnp.float32)
+    else:
+        wave = waves_ref[offset : offset + 1, 0:1]
     count, full = rmodes_ref.shape
     cols = full // 4
-    wave = table_ref[index_ref[0, offset]]
+    starts = list(range(0, count, CHUNK))
     rpos = rgeom_ref[...].astype(jnp.float32)
-    rflat = rmodes_ref[...].astype(jnp.float32).T
+    place = jnp.concatenate([rpos, jnp.zeros((5, count), jnp.float32)], axis=0).T
+    if plan.ready:
+        back_ref[...] = product(rboth_ref[...], near_ref[...], NN)
+    else:
+        rflat = rmodes_ref[...].astype(jnp.float32).T
     if plan.role == "own":
         spos, sflat = rpos, rflat
     else:
         spos = sgeom_ref[...].astype(jnp.float32)
         sflat = smodes_ref[...].astype(jnp.float32).T
-    rangle = wave * (rpos[0:1] + CHORD_SHIFT)
-    sangle = wave * spos[0:1]
+    angles = [wave * spos[0:1]]
+    if not plan.ready:
+        angles.append(wave * (rpos[0:1] + CHORD_SHIFT))
+    if plan.emits:
+        angles.append(waves_ref[offset + 1 : offset + 2, 0:1] * (rpos[0:1] + CHORD_SHIFT))
     quarter_turn = 0.5 * math.pi
     circle = cosine_of(
-        jnp.concatenate([rangle, rangle - quarter_turn, sangle, sangle - quarter_turn], axis=0)
-    )
-    recv = turned_modes(rflat, circle[0:1], circle[1:2])
-    send = turned_modes(sflat, circle[2:3], circle[3:4])
-    rhigh, rlow = halves(recv)
+        jnp.concatenate(angles + [angle - quarter_turn for angle in angles], axis=0)
+    )
+    turns = [(circle[k : k + 1], circle[len(angles) + k :][:1]) for k in range(len(angles))]
+
+    def receiving(turn):
+        high, low = halves(turned_modes(rflat, *turn))
+        both = jnp.concatenate([high, low[: 2 * cols]], axis=0)
+        return both, jnp.concatenate([crosswise(high), crosswise(low)], axis=0).T
+
+    def reciprocal(start, points):
+        part = slice(start, start + CHUNK)
+        dx = (place[part, 0:1] + CHORD_SHIFT) - points[0:1]
+        dy = place[part, 1:2] - points[1:2]
+        dz = place[part, 2:3] - points[2:3]
+        return lax.rsqrt(dx * dx + dy * dy + (dz * dz + CORE_SQUARE))
+
+    send = turned_modes(sflat, *turns[0])
     shigh, slow = halves(send)
-    rboth = jnp.concatenate([rhigh, rlow[: 2 * cols]], axis=0)
-    rows = jnp.concatenate([crosswise(rhigh), crosswise(rlow)], axis=0).T
+    if plan.ready:
+        rows = rows_ref[...]
+    else:
+        rboth, rows = receiving(turns[1])
     cross = crosswise(jnp.concatenate([shigh[2 * cols :], shigh[: 2 * cols]], axis=0))
     paired = jnp.concatenate([cross, cross], axis=0)
     srows = jnp.concatenate([shigh, slow[2 * cols :], slow[2 * cols :]], axis=0).T
@@ -120,48 +166,56 @@
     smom_rows = jnp.concatenate(
         [smom.astype(jnp.float32), jnp.zeros((full - 16, count), jnp.float32)], axis=0
     ).T.astype(jnp.bfloat16)
-    place = jnp.concatenate([rpos, jnp.zeros((5, count), jnp.float32)], axis=0).T
     lane = lax.broadcasted_iota(jnp.int32, (CHUNK, full), 1)
+
     def stage_l(start):
-        return product(rows[start:start+CHUNK], paired, NN)
+        return product(rows[start : start + CHUNK], paired, NN)
 
     def stage_v(start, along):
-        part = slice(start, start + CHUNK)
-        dx = (place[part, 0:1] + CHORD_SHIFT) - spos[0:1]
-        dy = place[part, 1:2] - spos[1:2]
-        dz = place[part, 2:3] - spos[2:3]
-        inverse = lax.rsqrt(dx * dx + dy * dy + (dz * dz + CORE_SQUARE))
-        kernel = inverse.astype(jnp.bfloat16)
+        if plan.ready:
+            part = slice(start, start + CHUNK)
+            return near_ref[part], (cube_ref[part] * along).astype(jnp.bfloat16)
+        inverse = reciprocal(start, spos)
         cubed = ((inverse * inverse) * (inverse * along)).astype(jnp.bfloat16)
-        return kernel, cubed
+        return inverse.astype(jnp.bfloat16), cubed
 
     def stage_m(start, kernel, cubed):
         part = slice(start, start + CHUNK)
         ahead = product(kernel, srows[:, :full], NN)
         moments = product(cubed, smom_rows, NN)
-        back = product(rboth[:, part], kernel, NN)
+        back = None if plan.ready else product(rboth[:, part], kernel, NN)
         backm = product(rmom[:, part], cubed, NN)
         both = rows[part].astype(jnp.float32)
         turn = jnp.sum((both[:, :full] + both[:, full:]) * ahead, axis=1, keepdims=True)
         row_ref[:, part] = jnp.where(lane == 4, turn, moments).T[:8]
         return back, backm
 
-    starts = list(range(0, count, CHUNK))
     along = stage_l(0)
     pair = stage_v(0, along)
     for k, start in enumerate(starts):
-        nxt = None
         if k + 1 < len(starts):
             along = stage_l(starts[k + 1])
         back, backm = stage_m(start, *pair)
         if k + 1 < len(starts):
             pair = stage_v(starts[k + 1], along)
         if k == 0:
-            back_ref[...] = back
             backm_ref[...] = backm
         else:
+            backm_ref[...] += backm
+        if plan.ready:
+            continue
+        if k == 0:
+            back_ref[...] = back
+        else:
             back_ref[...] += back
-            backm_ref[...] += backm
+    if plan.emits:
+        rboth_out[...], rows_out[...] = receiving(turns[2])
+        points = next_ref[...].astype(jnp.float32)
+        for start in starts:
+            part = slice(start, start + CHUNK)
+            inverse = reciprocal(start, points)
+            near_out[part] = inverse.astype(jnp.bfloat16)
+            cube_out[part] = inverse * inverse * inverse
     behind = back_ref[: full] + jnp.concatenate(
         [back_ref[full:], jnp.zeros((2 * cols, count), jnp.float32)], axis=0
     )
@@ -210,41 +264,63 @@
         force_ref[1] = force_imag
     else:
         grads[0][...] = held[0][...] + row
-        grads[1][...] = col
-        force_ref[0] = held[1][0] + force_real
-        force_ref[1] = held[1][1] + force_imag
+        if plan.last:
+            force_real = lanes_from(held[1][0] + force_real)
+            force_imag = lanes_from(held[1][1] + force_imag)
+            grads[1][...] = jnp.concatenate([col, force_real, force_imag], axis=0)
+        else:
+            grads[1][...] = col
+            force_ref[0] = held[1][0] + force_real
+            force_ref[1] = held[1][1] + force_imag
+
+
+def lanes_from(square):
+    side = square.shape[0]
+    wide = jnp.concatenate([square[at : at + 8] for at in range(0, side, 8)], axis=1)
+    return jnp.concatenate([wide[c : c + 1] for c in range(8)], axis=1)
 
 
 class Plan:
-    def __init__(self, role, grad_scale, force_scale):
+    def __init__(self, role, last, emits, ready, grad_scale, force_scale):
         self.role = role
+        self.last = last
+        self.emits = emits
+        self.ready = ready
         self.grad_scale = grad_scale
         self.force_scale = force_scale
         self.held = 0 if role == "own" else 2
         self.grads = 1 if role == "own" else 2
 
 
-def tile_terms(offset, plan, table, index, recv, send, *held):
+def tile_terms(offset, plan, lead, recv, *operands):
     count, width = recv[1].shape
     cols = width // 4
-    smem = pl.BlockSpec(memory_space=pltpu.SMEM)
     vmem = pl.BlockSpec(memory_space=pltpu.VMEM)
     grad = jax.ShapeDtypeStruct((3, count), jnp.float32)
     force = jax.ShapeDtypeStruct((2, cols, cols), jnp.float32)
-    operands = [vmem] * 4
+    source = vmem
     extra = []
-    if plan.role == "own":
-        operands = [pl.BlockSpec(memory_space=pl.ANY)] * 4
-        extra = [
-            pltpu.VMEM(recv[0].shape, recv[0].dtype),
-            pltpu.VMEM(recv[1].shape, recv[1].dtype),
-            pltpu.SemaphoreType.DMA((2,)),
-        ]
+    outs = (grad,) * plan.grads + (force,)
+    if plan.last:
+        outs = (grad, jax.ShapeDtypeStruct((5, count), jnp.float32))
+    if plan.role == "own":
+        source = pl.BlockSpec(memory_space=pltpu.HBM)
+        extra = [pltpu.SMEM(part.shape, part.dtype) for part in lead]
+        extra.append(pltpu.SemaphoreType.DMA((4,)))
+        outs += (pltpu.VMEM((8, width), jnp.float32),)
+        outs += tuple(pltpu.VMEM(part.shape, part.dtype) for part in recv)
+    if plan.emits:
+        outs += (
+            pltpu.VMEM((count, count), jnp.bfloat16),
+            pltpu.VMEM((count, count), jnp.float32),
+            pltpu.VMEM((count, 2 * width), jnp.bfloat16),
+            pltpu.VMEM((width + 2 * cols, count), jnp.bfloat16),
+        )
     return pl.pallas_call(
         functools.partial(tile_kernel, offset, plan),
-        out_shape=(grad,) * plan.grads + (force,),
-        in_specs=[smem, smem] + operands + [vmem] * plan.held,
-        out_specs=(vmem,) * (plan.grads + 1),
+        out_shape=outs,
+        in_specs=[source] * (len(lead) + 2) + [vmem] * len(operands),
+        out_specs=(vmem,) * len(outs),
         scratch_shapes=[
             pltpu.VMEM((width + 2 * cols, count), jnp.float32),
             pltpu.VMEM((16, count), jnp.float32),
@@ -252,13 +328,13 @@
         ]
         + extra,
         name="tile_%d" % offset,
-        compiler_params=pltpu.CompilerParams(vmem_limit_bytes=48 << 20),
+        compiler_params=pltpu.CompilerParams(vmem_limit_bytes=40 << 20),
         cost_estimate=pl.CostEstimate(
             flops=2 * count * count * width * 6,
             transcendentals=count * count,
             bytes_accessed=4 * count * width,
         ),
-    )(table, index, *recv, *send, *held)
+    )(*lead, *recv, *operands)
 
 
 def local(geometry, modes, reduced_freq, freq_index):
@@ -271,35 +347,51 @@
     grad_scale = 1.0 / math.sqrt(columns * steps * row_count * freqs)
     force_scale = 1.0 / math.sqrt(row_count * row_count * blocks * steps)
 
-    def terms(offset, *operands):
-        plan = Plan("sent" if offset else "own", grad_scale, force_scale)
-        return tile_terms(offset, plan, reduced_freq, freq_index, *operands)
-
-    sender = passed_along(own, "blk", 1)
-    mine, force = terms(0, own, own)
-    sender, mine = lax.optimization_barrier((sender, mine))
+    def terms(offset, lead, recv, *operands):
+        role = "sent" if offset else "own"
+        plan = Plan(role, offset == steps - 1, 0 < offset < steps - 1, offset > 1, grad_scale, force_scale)
+        return tile_terms(offset, plan, lead, recv, *operands)
+
+    block = passed_along(own[1], "blk", 1)
+    points = [passed_along(own[0], "blk", offset) for offset in range(1, steps)]
+    placed = [
+        pltpu.with_memory_space_constraint(part, pltpu.HBM)
+        for part in (reduced_freq, freq_index, *own)
+    ]
+    mine, force, waves, *kept = terms(0, placed[:2], placed[2:])
+    block, points, mine = lax.optimization_barrier((block, points, mine))
     returned = []
+    prepared = []
     for offset in range(1, steps):
-        current = sender
+        current = block
+        extra = prepared
         if offset + 1 < steps:
-            sender = passed_along(current, "blk", 1)
-        mine, back, force = terms(offset, own, current, mine, force)
+            block = passed_along(block, "blk", 1)
+            extra = [points[offset]] + extra
+        mine, back, *prepared = terms(
+            offset, [waves], kept, points[offset - 1], current, *extra, mine, force
+        )
         returned.append(passed_along(back, "blk", -offset))
+        force = prepared.pop(0) if prepared else back[3:]
     total = mine
     for back in returned:
-        total = total + back
-    if blocks == 4:
-        pair = force + passed_along(force, "blk", -2)
+        total = total + back[:3]
+    if blocks == 4 and steps == 3:
+        pair = force + returned[-1][3:]
         force_total = pair + exchanged(pair, "blk", 1)
     else:
         force_total = lax.psum(force, "blk")
-    share = row_count // freqs
     place = lax.axis_index("freq")
-    result = lax.dynamic_slice_in_dim(total, place * share, share, axis=1)
-    for flip in range(1, freqs):
-        piece = lax.dynamic_slice_in_dim(total, (place ^ flip) * share, share, axis=1)
-        result = result + exchanged(piece, "freq", flip)
-    return (result, force_total[None])
+    flip = freqs // 2
+    while flip:
+        half = total.shape[1] // 2
+        side = (place // flip) % 2
+        kept = lax.dynamic_slice_in_dim(total, side * half, half, axis=1)
+        sent = lax.dynamic_slice_in_dim(total, (1 - side) * half, half, axis=1)
+        total = kept + exchanged(sent, "freq", flip)
+        flip //= 2
+    force_total = force_total.reshape(2, 8, columns // 8, columns).transpose(0, 2, 1, 3)
+    return (total, force_total.reshape(1, 2, columns, columns))
 
 
 def solution(mesh):

time: 38.2 us -> 36.3 us (0.950)
  starting transfers between devices: 14.3 us -> 9.46 us
  waiting for transfers between devices: 6.33 us -> 10.9 us
  local copies, waits for them, and re-layouts: 1.67 us -> 0.73 us
  other arithmetic: 1.23 us -> 0.62 us
    ppermute x7 -> x6, starting transfers between devices: 12.3 us -> 7.34 us  [passed_along(): return lax.ppermute(value, axis, pairs)]
    ppermute x7 -> x6, waiting for transfers between devices: 3.03 us -> 8 us  [passed_along(): return lax.ppermute(value, axis, pairs)]
    unnamed x8 -> x0, local copies, waits for them, and re-layouts: 1.66 us -> none
    broadcast_in_dim x1 -> x0, other arithmetic: 0.62 us -> none  [local(): return (result, force_total[None])]
    transpose x0 -> x1, local copies, waits for them, and re-layouts: none -> 0.62 us  [local(): force_total.reshape(2, 8, columns // 8, columns).transpose(0, 2, 1, 3)]
    ppermute x4 -> x3, waiting for transfers between devices: 3.29 us -> 2.88 us  [exchanged(): return lax.ppermute(value, axis, pairs)]
    ppermute x4 -> x3, starting transfers between devices: 2 us -> 2.12 us  [exchanged(): return lax.ppermute(value, axis, pairs)]
  transfers between devices with their start and end apart: 11 -> 9, of which waited for: 6 -> 7; matrix products, arithmetic and copies ran while one was open for 2% -> 2% of each run, Pallas kernels for 36% -> 30%
where the time goes in v4:
time: 36.3 us; the launch traced here: 36.1 us
  Pallas kernels  13.7 us (38%)
  waiting for transfers between devices  10.9 us (30%)
  starting transfers between devices  9.46 us (26%)
  local copies, waits for them, and re-layouts  0.73 us (2%)
  between operations  0.7 us (2%)
  other arithmetic  0.62 us (2%)
    pallas_call x3, Pallas kernels, tile_terms(): pl.pallas_call(functools.partial(tile_kernel, offset, plan), out_shape=ou...  13.7 us
    ppermute x6, waiting for transfers between devices, passed_along(): return lax.ppermute(value, axis, pairs)  8 us
    ppermute x6, starting transfers between devices, passed_along(): return lax.ppermute(value, axis, pairs)  7.34 us
    ppermute x3, waiting for transfers between devices, exchanged(): return lax.ppermute(value, axis, pairs)  2.88 us
    ppermute x3, starting transfers between devices, exchanged(): return lax.ppermute(value, axis, pairs)  2.12 us
  transfers between devices with their start and end apart: 9, of which 7 were waited for; matrix products, arithmetic and copies ran while one was open for 2% of the time, Pallas kernels for 30%

profile of v4, /device:TPU:0, one launch (start us, length us, event | category | flops | bytes accessed | tf_op | source)
XLA Modules:
  0.0 36.1 jit_solution(717948710207024861)
XLA Ops:
  0.6 3.1 %collective-permute-start = (bf16[1024,128]{1,0:T(8,128)(2,1)}, bf16[1024,128]{1,0:T(8,128)(2,1)S(1)}, u32[]{:S(2)}, u32[]{:S(2)}) collective-permute-start(bf16[1024,128]{1,0:T(8,128)(2,1)} %bitcast.7), channel_id=1, source_target_pairs={{0,4},{4,8},{8,12},{12,0},{1,5},{5,9},{9,13},{13,1},{2,6},{6,10},{... | collective-permute-start | bytes 786440 | tf_op jit(solution)/shard_map/ppermute | solution.py:22
  3.7 1.6 %collective-permute-start.1 = (bf16[3,1024]{1,0:T(4,128)(2,1)}, bf16[3,1024]{1,0:T(4,128)(2,1)S(1)}, u32[]{:S(2)}, u32[]{:S(2)}) collective-permute-start(bf16[3,1024]{1,0:T(4,128)(2,1)} %refs_2_.1), channel_id=1, source_target_pairs={{0,4},{4,8},{8,12},{12,0},{1,5},{5,9},{9,13},{13,1},{2,6},{6,10},{... | collective-permute-start | bytes 18440 | tf_op jit(solution)/shard_map/ppermute | solution.py:22
  5.3 1.1 %collective-permute-start.2 = (bf16[3,1024]{1,0:T(4,128)(2,1)}, bf16[3,1024]{1,0:T(4,128)(2,1)S(1)}, u32[]{:S(2)}, u32[]{:S(2)}) collective-permute-start(bf16[3,1024]{1,0:T(4,128)(2,1)} %refs_2_.1), channel_id=1, source_target_pairs={{0,8},{4,12},{8,0},{12,4},{1,9},{5,13},{9,1},{13,5},{2,10},{6,14},... | collective-permute-start | bytes 18440 | tf_op jit(solution)/shard_map/ppermute | solution.py:22
  6.4 4.9 %tile_0.1 = (f32[3,1024]{1,0:T(4,128)S(1)}, f32[2,32,32]{2,1,0:T(8,128)S(1)}, f32[8,128]{1,0:T(8,128)S(1)}, bf16[3,1024]{1,0:T(4,128)(2,1)S(1)}, bf16[1024,128]{1,0:T(8,128)(2,1)S(1)}) custom-call(f32[16]{0:T(128)} %refs_0_.1, s32[1,3]{1,0:T(1,128)} %refs_1_.1, bf16[3,1024]{1,0:T(4,128)(2,1)} %refs_2_.1, bf16[1024,128]{1,0:T(8,128)(2,1)} %bitcast.8), custom_call_target="tpu_custom_call" | custom-call | flops 1610612736 | bytes 524288 | tf_op jit(solution)/shard_map/tile_0/pallas_call | solution.py:319
  11.3 1.4 %collective-permute-done.1.refs_3_ = bf16[3,1024]{1,0:T(4,128)(2,1)S(1)} collective-permute-done((bf16[3,1024]{1,0:T(4,128)(2,1)}, bf16[3,1024]{1,0:T(4,128)(2,1)S(1)}, u32[]{:S(2)}, u32[]{:S(2)}) %collective-permute-start.1) | collective-permute-done | bytes 6176 | tf_op jit(solution)/shard_map/ppermute | solution.py:22
  12.6 0.2 collective-permute-done.2.refs_5_.refs_3_
  12.8 0.0 collective-permute-done.refs_4_
  12.8 0.5 %collective-permute-start.3 = (bf16[1024,128]{1,0:T(8,128)(2,1)S(1)}, bf16[1024,128]{1,0:T(8,128)(2,1)S(1)}, u32[]{:S(2)}, u32[]{:S(2)}) collective-permute-start(bf16[1024,128]{1,0:T(8,128)(2,1)S(1)} %collective-permute-done.refs_4_), channel_id=1, source_target_pairs={{0,4},{4,8},{8,12},{12,0},{1,5},{5,9},{9,13},{13,1},{2,6},{6,10},{... | collective-permute-start | bytes 786440 | tf_op jit(solution)/shard_map/ppermute | solution.py:22
  13.3 5.8 %tile_1.1 = (f32[3,1024]{1,0:T(4,128)S(1)}, f32[3,1024]{1,0:T(4,128)S(1)}, f32[2,32,32]{2,1,0:T(8,128)S(1)}, bf16[1024,1024]{1,0:T(8,128)(2,1)S(1)}, f32[1024,10...) custom-call(f32[8,128]{1,0:T(8,128)S(1)} %get-tuple-element.20.refs_0_, ...), custom_call_target="tpu_custom_call" | custom-call | flops 1610612736 | bytes 524288 | tf_op jit(solution)/shard_map/tile_1/pallas_call | solution.py:319
  19.0 2.7 %collective-permute-done.3.refs_4_ = bf16[1024,128]{1,0:T(8,128)(2,1)S(1)} collective-permute-done((bf16[1024,128]{1,0:T(8,128)(2,1)S(1)}, bf16[1024,128]{1,0:T(8,128)(2,1)S(1)}, u32[]{:S(2)}, u32[]{:S(2)}) %collective-permute-start.3) | collective-permute-done | bytes 262176 | tf_op jit(solution)/shard_map/ppermute | solution.py:22
  21.8 3.1 %tile_2.1 = (f32[3,1024]{1,0:T(4,128)S(1)}, f32[5,1024]{1,0:T(8,128)S(1)}) custom-call(f32[8,128]{1,0:T(8,128)S(1)} %get-tuple-element.20.refs_0_, bf16[3,1024]{1,0:T(4,128)(2,1)S(1)} %get-tuple-element.21.refs_1_, bf16[1024,128]{1,0:T(8,128)(2,1)S(1)} %get-tuple-element.22.refs_2_, bf16[3,1024]{1,0:T(4,128)(2,1)S(1)} %collective-permute-done.2.refs_5_.refs_3_, ...), custom_call_target="tpu_custom_call" | custom-call | flops 1610612736 | bytes 524288 | tf_op jit(solution)/shard_map/tile_2/pallas_call | solution.py:319
  24.9 0.1 collective-permute-start.5
  24.9 1.0 %collective-permute-start.4 = (f32[3,1024]{1,0:T(4,128)S(1)}, f32[3,1024]{1,0:T(4,128)S(1)}, u32[]{:S(2)}, u32[]{:S(2)}) collective-permute-start(f32[3,1024]{1,0:T(4,128)S(1)} %get-tuple-element.36), channel_id=1, source_target_pairs={{0,12},{4,0},{8,4},{12,8},{1,13},{5,1},{9,5},{13,9},{2,14},{6,2},{... | collective-permute-start | bytes 36872 | tf_op jit(solution)/shard_map/ppermute | solution.py:22
  26.0 2.7 %collective-permute-done.4 = f32[3,1024]{1,0:T(4,128)S(1)} collective-permute-done((f32[3,1024]{1,0:T(4,128)S(1)}, f32[3,1024]{1,0:T(4,128)S(1)}, u32[]{:S(2)}, u32[]{:S(2)}) %collective-permute-start.4) | collective-permute-done | bytes 12320 | tf_op jit(solution)/shard_map/ppermute | solution.py:22
  28.7 1.0 %collective-permute-done.5 = f32[5,1024]{1,0:T(8,128)S(1)} collective-permute-done((f32[5,1024]{1,0:T(8,128)S(1)}, f32[5,1024]{1,0:T(8,128)S(1)}, u32[]{:S(2)}, u32[]{:S(2)}) %collective-permute-start.5) | collective-permute-done | bytes 20512 | tf_op jit(solution)/shard_map/ppermute | solution.py:22
  29.8 1.3 %collective-permute-start.6 = (f32[3,512]{1,0:T(4,128)S(1)}, f32[3,512]{1,0:T(4,128)S(1)}, u32[]{:S(2)}, u32[]{:S(2)}) collective-permute-start(f32[3,512]{1,0:T(4,128)S(1)} %constant_dynamic-slice_fusion.1), channel_id=1, source_target_pairs={{0,2},{1,3},{2,0},{3,1},{4,6},{5,7},{6,4},{7,5},{8,10},{9,11},{10,... | collective-permute-start | bytes 18440 | tf_op jit(solution)/shard_map/ppermute | solution.py:27
  31.1 0.8 %collective-permute-start.8 = (f32[2,1024]{1,0:T(2,128)S(1)}, f32[2,1024]{1,0:T(2,128)S(1)}, u32[]{:S(2)}, u32[]{:S(2)}) collective-permute-start(f32[2,1024]{1,0:T(2,128)S(1)} %slice_add_fusion.1), channel_id=1, source_target_pairs={{0,4},{4,0},{8,12},{12,8},{1,5},{5,1},{9,13},{13,9},{2,6},{6,2},{1... | collective-permute-start | bytes 24584 | tf_op jit(solution)/shard_map/ppermute | solution.py:27
  31.9 1.6 %collective-permute-done.6 = f32[3,512]{1,0:T(4,128)S(1)} collective-permute-done((f32[3,512]{1,0:T(4,128)S(1)}, f32[3,512]{1,0:T(4,128)S(1)}, u32[]{:S(2)}, u32[]{:S(2)}) %collective-permute-start.6) | collective-permute-done | bytes 6176 | tf_op jit(solution)/shard_map/ppermute | solution.py:27
  33.5 0.0 collective-permute-start.7
  33.5 1.3 %collective-permute-done.8 = f32[2,1024]{1,0:T(2,128)S(1)} collective-permute-done((f32[2,1024]{1,0:T(2,128)S(1)}, f32[2,1024]{1,0:T(2,128)S(1)}, u32[]{:S(2)}, u32[]{:S(2)}) %collective-permute-start.8) | collective-permute-done | bytes 8224 | tf_op jit(solution)/shard_map/ppermute | solution.py:27
  34.8 0.1 reshape.10
  34.9 0.6 %copy.8 = f32[2,4,8,32]{3,2,1,0:T(8,128)} copy(f32[2,4,8,32]{3,1,2,0:T(4,128)S(1)} %bitcast.5) | data formatting | bytes 16384 | tf_op jit(solution)/shard_map/transpose | solution.py:393
  35.5 0.0 collective-permute-done.7
  35.5 0.6 %dynamic-slice_add_fusion.1 = f32[3,256]{1,0:T(4,128)} fusion(f32[3,256]{1,0:T(4,128)S(1)} %collective-permute-done.7, f32[3,512]{1,0:T(4,128)S(1)} %dynamic-slice_add_fusion, s32[]{:T(128)S(6)} %select_n.33), kind=kLoop, calls=%fused_computation.4 | loop fusion | flops 768 | bytes 9220 | tf_op jit(solution)/shard_map/add | solution.py:391
  (6 shorter events, 0.0 us)
Async XLA Ops:
  0.6 12.1 %collective-permute-start = (bf16[1024,128]{1,0:T(8,128)(2,1)}, bf16[1024,128]{1,0:T(8,128)(2,1)S(1)}, u32[]{:S(2)}, u32[]{:S(2)}) collective-permute-start(bf16[1024,128]{1,0:T(8,128)(2,1)} %bitcast.7), channel_id=1, source_target_pairs={{0,4},{4,8},{8,12},{12,0},{1,5},{5,9},{9,13},{13,1},{2,6},{6,10},{... | collective-permute-start | bytes 786440 | tf_op jit(solution)/shard_map/ppermute | solution.py:22
  3.7 8.9 %collective-permute-start.1 = (bf16[3,1024]{1,0:T(4,128)(2,1)}, bf16[3,1024]{1,0:T(4,128)(2,1)S(1)}, u32[]{:S(2)}, u32[]{:S(2)}) collective-permute-start(bf16[3,1024]{1,0:T(4,128)(2,1)} %refs_2_.1), channel_id=1, source_target_pairs={{0,4},{4,8},{8,12},{12,0},{1,5},{5,9},{9,13},{13,1},{2,6},{6,10},{... | collective-permute-start | bytes 18440 | tf_op jit(solution)/shard_map/ppermute | solution.py:22
  5.3 7.5 %collective-permute-start.2 = (bf16[3,1024]{1,0:T(4,128)(2,1)}, bf16[3,1024]{1,0:T(4,128)(2,1)S(1)}, u32[]{:S(2)}, u32[]{:S(2)}) collective-permute-start(bf16[3,1024]{1,0:T(4,128)(2,1)} %refs_2_.1), channel_id=1, source_target_pairs={{0,8},{4,12},{8,0},{12,4},{1,9},{5,13},{9,1},{13,5},{2,10},{6,14},... | collective-permute-start | bytes 18440 | tf_op jit(solution)/shard_map/ppermute | solution.py:22
  12.8 9.0 %collective-permute-start.3 = (bf16[1024,128]{1,0:T(8,128)(2,1)S(1)}, bf16[1024,128]{1,0:T(8,128)(2,1)S(1)}, u32[]{:S(2)}, u32[]{:S(2)}) collective-permute-start(bf16[1024,128]{1,0:T(8,128)(2,1)S(1)} %collective-permute-done.refs_4_), channel_id=1, source_target_pairs={{0,4},{4,8},{8,12},{12,0},{1,5},{5,9},{9,13},{13,1},{2,6},{6,10},{... | collective-permute-start | bytes 786440 | tf_op jit(solution)/shard_map/ppermute | solution.py:22
  24.9 4.9 %collective-permute-start.5 = (f32[5,1024]{1,0:T(8,128)S(1)}, f32[5,1024]{1,0:T(8,128)S(1)}, u32[]{:S(2)}, u32[]{:S(2)}) collective-permute-start(f32[5,1024]{1,0:T(8,128)S(1)} %get-tuple-element.37), channel_id=1, source_target_pairs={{0,8},{4,12},{8,0},{12,4},{1,9},{5,13},{9,1},{13,5},{2,10},{6,14},... | collective-permute-start | bytes 61448 | tf_op jit(solution)/shard_map/ppermute | solution.py:22
  24.9 3.8 %collective-permute-start.4 = (f32[3,1024]{1,0:T(4,128)S(1)}, f32[3,1024]{1,0:T(4,128)S(1)}, u32[]{:S(2)}, u32[]{:S(2)}) collective-permute-start(f32[3,1024]{1,0:T(4,128)S(1)} %get-tuple-element.36), channel_id=1, source_target_pairs={{0,12},{4,0},{8,4},{12,8},{1,13},{5,1},{9,5},{13,9},{2,14},{6,2},{... | collective-permute-start | bytes 36872 | tf_op jit(solution)/shard_map/ppermute | solution.py:22
  29.8 3.7 %collective-permute-start.6 = (f32[3,512]{1,0:T(4,128)S(1)}, f32[3,512]{1,0:T(4,128)S(1)}, u32[]{:S(2)}, u32[]{:S(2)}) collective-permute-start(f32[3,512]{1,0:T(4,128)S(1)} %constant_dynamic-slice_fusion.1), channel_id=1, source_target_pairs={{0,2},{1,3},{2,0},{3,1},{4,6},{5,7},{6,4},{7,5},{8,10},{9,11},{10,... | collective-permute-start | bytes 18440 | tf_op jit(solution)/shard_map/ppermute | solution.py:27
  31.1 3.7 %collective-permute-start.8 = (f32[2,1024]{1,0:T(2,128)S(1)}, f32[2,1024]{1,0:T(2,128)S(1)}, u32[]{:S(2)}, u32[]{:S(2)}) collective-permute-start(f32[2,1024]{1,0:T(2,128)S(1)} %slice_add_fusion.1), channel_id=1, source_target_pairs={{0,4},{4,0},{8,12},{12,8},{1,5},{5,1},{9,13},{13,9},{2,6},{6,2},{1... | collective-permute-start | bytes 24584 | tf_op jit(solution)/shard_map/ppermute | solution.py:27
  33.5 2.0 %collective-permute-start.7 = (f32[3,256]{1,0:T(4,128)S(1)}, f32[3,256]{1,0:T(4,128)S(1)}, u32[]{:S(2)}, u32[]{:S(2)}) collective-permute-start(f32[3,256]{1,0:T(4,128)S(1)} %constant_dynamic-slice_fusion), channel_id=1, source_target_pairs={{0,1},{1,0},{2,3},{3,2},{4,5},{5,4},{6,7},{7,6},{8,9},{9,8},{10,11... | collective-permute-start | bytes 9224 | tf_op jit(solution)/shard_map/ppermute | solution.py:27

commit v5 on v4

--- a/solution.py
+++ b/solution.py
@@ -73,6 +73,12 @@
     ).astype(jnp.bfloat16)
 
 
+def moment_columns(pos, width):
+    rows = moment_rows(pos).astype(jnp.float32)
+    still = jnp.zeros((width - rows.shape[0], pos.shape[1]), jnp.float32)
+    return jnp.concatenate([rows, still], axis=0).T.astype(jnp.bfloat16)
+
+
 def tile_kernel(offset, plan, *refs):
     refs = list(refs)
 
@@ -86,7 +92,7 @@
     if plan.emits:
         (next_ref,) = taken(1)
     if plan.ready:
-        near_ref, cube_ref, rows_ref, rboth_ref = taken(4)
+        near_ref, cube_ref, rows_ref, behind_ref, smom_ref = taken(5)
     held = taken(plan.held)
     grads = taken(plan.grads)
     if not plan.last:
@@ -94,8 +100,10 @@
     if plan.role == "own":
         waves_out, geom_out, modes_out = taken(3)
     if plan.emits:
-        near_out, cube_out, rows_out, rboth_out = taken(4)
+        near_out, cube_out, rows_out, behind_out, smom_out = taken(5)
     back_ref, backm_ref, row_ref = taken(3)
+    if plan.ready:
+        back_ref = behind_ref
     if plan.role == "own":
         table_buf, index_buf, sems = taken(3)
         copies = [
@@ -120,9 +128,7 @@
     starts = list(range(0, count, CHUNK))
     rpos = rgeom_ref[...].astype(jnp.float32)
     place = jnp.concatenate([rpos, jnp.zeros((5, count), jnp.float32)], axis=0).T
-    if plan.ready:
-        back_ref[...] = product(rboth_ref[...], near_ref[...], NN)
-    else:
+    if not plan.ready:
         rflat = rmodes_ref[...].astype(jnp.float32).T
     if plan.role == "own":
         spos, sflat = rpos, rflat
@@ -162,10 +168,7 @@
     paired = jnp.concatenate([cross, cross], axis=0)
     srows = jnp.concatenate([shigh, slow[2 * cols :], slow[2 * cols :]], axis=0).T
     rmom = moment_rows(rpos)
-    smom = moment_rows(spos)
-    smom_rows = jnp.concatenate(
-        [smom.astype(jnp.float32), jnp.zeros((full - 16, count), jnp.float32)], axis=0
-    ).T.astype(jnp.bfloat16)
+    smom_rows = smom_ref[...] if plan.ready else moment_columns(spos, full)
     lane = lax.broadcasted_iota(jnp.int32, (CHUNK, full), 1)
 
     def stage_l(start):
@@ -209,13 +212,15 @@
         else:
             back_ref[...] += back
     if plan.emits:
-        rboth_out[...], rows_out[...] = receiving(turns[2])
+        rboth, rows_out[...] = receiving(turns[2])
         points = next_ref[...].astype(jnp.float32)
         for start in starts:
             part = slice(start, start + CHUNK)
             inverse = reciprocal(start, points)
             near_out[part] = inverse.astype(jnp.bfloat16)
             cube_out[part] = inverse * inverse * inverse
+        behind_out[...] = product(rboth, near_out[...], NN)
+        smom_out[...] = moment_columns(points, full)
     behind = back_ref[: full] + jnp.concatenate(
         [back_ref[full:], jnp.zeros((2 * cols, count), jnp.float32)], axis=0
     )
@@ -314,7 +319,8 @@
             pltpu.VMEM((count, count), jnp.bfloat16),
             pltpu.VMEM((count, count), jnp.float32),
             pltpu.VMEM((count, 2 * width), jnp.bfloat16),
-            pltpu.VMEM((width + 2 * cols, count), jnp.bfloat16),
+            pltpu.VMEM((width + 2 * cols, count), jnp.float32),
+            pltpu.VMEM((count, width), jnp.bfloat16),
         )
     return pl.pallas_call(
         functools.partial(tile_kernel, offset, plan),

time: 36.3 us -> 36 us (level)
  no operation moved by 1% of the time
where the time goes in v5:
time: 36 us; the launch traced here: 35.8 us
  Pallas kernels  13.4 us (37%)
  waiting for transfers between devices  10.9 us (30%)
  starting transfers between devices  9.46 us (26%)
  local copies, waits for them, and re-layouts  0.73 us (2%)
  between operations  0.69 us (2%)
  other arithmetic  0.62 us (2%)
    pallas_call x3, Pallas kernels, tile_terms(): pl.pallas_call(functools.partial(tile_kernel, offset, plan), out_shape=ou...  13.4 us
    ppermute x6, waiting for transfers between devices, passed_along(): return lax.ppermute(value, axis, pairs)  7.99 us
    ppermute x6, starting transfers between devices, passed_along(): return lax.ppermute(value, axis, pairs)  7.34 us
    ppermute x3, waiting for transfers between devices, exchanged(): return lax.ppermute(value, axis, pairs)  2.88 us
    ppermute x3, starting transfers between devices, exchanged(): return lax.ppermute(value, axis, pairs)  2.12 us
  transfers between devices with their start and end apart: 9, of which 7 were waited for; matrix products, arithmetic and copies ran while one was open for 2% of the time, Pallas kernels for 30%

profile of v5, /device:TPU:0, one launch (start us, length us, event | category | flops | bytes accessed | tf_op | source)
XLA Modules:
  0.0 35.8 jit_solution(4457561508459350417)
XLA Ops:
  0.6 3.1 %collective-permute-start = (bf16[1024,128]{1,0:T(8,128)(2,1)}, bf16[1024,128]{1,0:T(8,128)(2,1)S(1)}, u32[]{:S(2)}, u32[]{:S(2)}) collective-permute-start(bf16[1024,128]{1,0:T(8,128)(2,1)} %bitcast.7), channel_id=1, source_target_pairs={{0,4},{4,8},{8,12},{12,0},{1,5},{5,9},{9,13},{13,1},{2,6},{6,10},{... | collective-permute-start | bytes 786440 | tf_op jit(solution)/shard_map/ppermute | solution.py:22
  3.7 1.6 %collective-permute-start.1 = (bf16[3,1024]{1,0:T(4,128)(2,1)}, bf16[3,1024]{1,0:T(4,128)(2,1)S(1)}, u32[]{:S(2)}, u32[]{:S(2)}) collective-permute-start(bf16[3,1024]{1,0:T(4,128)(2,1)} %refs_2_.1), channel_id=1, source_target_pairs={{0,4},{4,8},{8,12},{12,0},{1,5},{5,9},{9,13},{13,1},{2,6},{6,10},{... | collective-permute-start | bytes 18440 | tf_op jit(solution)/shard_map/ppermute | solution.py:22
  5.3 1.1 %collective-permute-start.2 = (bf16[3,1024]{1,0:T(4,128)(2,1)}, bf16[3,1024]{1,0:T(4,128)(2,1)S(1)}, u32[]{:S(2)}, u32[]{:S(2)}) collective-permute-start(bf16[3,1024]{1,0:T(4,128)(2,1)} %refs_2_.1), channel_id=1, source_target_pairs={{0,8},{4,12},{8,0},{12,4},{1,9},{5,13},{9,1},{13,5},{2,10},{6,14},... | collective-permute-start | bytes 18440 | tf_op jit(solution)/shard_map/ppermute | solution.py:22
  6.4 4.9 %tile_0.1 = (f32[3,1024]{1,0:T(4,128)S(1)}, f32[2,32,32]{2,1,0:T(8,128)S(1)}, f32[8,128]{1,0:T(8,128)S(1)}, bf16[3,1024]{1,0:T(4,128)(2,1)S(1)}, bf16[1024,128]{1,0:T(8,128)(2,1)S(1)}) custom-call(f32[16]{0:T(128)} %refs_0_.1, s32[1,3]{1,0:T(1,128)} %refs_1_.1, bf16[3,1024]{1,0:T(4,128)(2,1)} %refs_2_.1, bf16[1024,128]{1,0:T(8,128)(2,1)} %bitcast.8), custom_call_target="tpu_custom_call" | custom-call | flops 1610612736 | bytes 524288 | tf_op jit(solution)/shard_map/tile_0/pallas_call | solution.py:325
  11.3 1.4 %collective-permute-done.1.refs_3_ = bf16[3,1024]{1,0:T(4,128)(2,1)S(1)} collective-permute-done((bf16[3,1024]{1,0:T(4,128)(2,1)}, bf16[3,1024]{1,0:T(4,128)(2,1)S(1)}, u32[]{:S(2)}, u32[]{:S(2)}) %collective-permute-start.1) | collective-permute-done | bytes 6176 | tf_op jit(solution)/shard_map/ppermute | solution.py:22
  12.6 0.2 collective-permute-done.2.refs_5_.refs_3_
  12.8 0.0 collective-permute-done.refs_4_
  12.8 0.5 %collective-permute-start.3 = (bf16[1024,128]{1,0:T(8,128)(2,1)S(1)}, bf16[1024,128]{1,0:T(8,128)(2,1)S(1)}, u32[]{:S(2)}, u32[]{:S(2)}) collective-permute-start(bf16[1024,128]{1,0:T(8,128)(2,1)S(1)} %collective-permute-done.refs_4_), channel_id=1, source_target_pairs={{0,4},{4,8},{8,12},{12,0},{1,5},{5,9},{9,13},{13,1},{2,6},{6,10},{... | collective-permute-start | bytes 786440 | tf_op jit(solution)/shard_map/ppermute | solution.py:22
  13.3 5.8 %tile_1.1 = (f32[3,1024]{1,0:T(4,128)S(1)}, f32[3,1024]{1,0:T(4,128)S(1)}, f32[2,32,32]{2,1,0:T(8,128)S(1)}, bf16[1024,1024]{1,0:T(8,128)(2,1)S(1)}, f32[1024,10...) custom-call(f32[8,128]{1,0:T(8,128)S(1)} %get-tuple-element.21.refs_0_, ...), custom_call_target="tpu_custom_call" | custom-call | flops 1610612736 | bytes 524288 | tf_op jit(solution)/shard_map/tile_1/pallas_call | solution.py:325
  19.0 2.7 %collective-permute-done.3.refs_4_ = bf16[1024,128]{1,0:T(8,128)(2,1)S(1)} collective-permute-done((bf16[1024,128]{1,0:T(8,128)(2,1)S(1)}, bf16[1024,128]{1,0:T(8,128)(2,1)S(1)}, u32[]{:S(2)}, u32[]{:S(2)}) %collective-permute-start.3) | collective-permute-done | bytes 262176 | tf_op jit(solution)/shard_map/ppermute | solution.py:22
  21.8 2.8 %tile_2.1 = (f32[3,1024]{1,0:T(4,128)S(1)}, f32[5,1024]{1,0:T(8,128)S(1)}) custom-call(f32[8,128]{1,0:T(8,128)S(1)} %get-tuple-element.21.refs_0_, bf16[3,1024]{1,0:T(4,128)(2,1)S(1)} %get-tuple-element.22.refs_1_, bf16[1024,128]{1,0:T(8,128)(2,1)S(1)} %get-tuple-element.23.refs_2_, bf16[3,1024]{1,0:T(4,128)(2,1)S(1)} %collective-permute-done.2.refs_5_.refs_3_, ...), custom_call_target="tpu_custom_call" | custom-call | flops 1610612736 | bytes 524288 | tf_op jit(solution)/shard_map/tile_2/pallas_call | solution.py:325
  24.5 0.1 collective-permute-start.5
  24.6 1.0 %collective-permute-start.4 = (f32[3,1024]{1,0:T(4,128)S(1)}, f32[3,1024]{1,0:T(4,128)S(1)}, u32[]{:S(2)}, u32[]{:S(2)}) collective-permute-start(f32[3,1024]{1,0:T(4,128)S(1)} %get-tuple-element.38), channel_id=1, source_target_pairs={{0,12},{4,0},{8,4},{12,8},{1,13},{5,1},{9,5},{13,9},{2,14},{6,2},{... | collective-permute-start | bytes 36872 | tf_op jit(solution)/shard_map/ppermute | solution.py:22
  25.6 2.7 %collective-permute-done.4 = f32[3,1024]{1,0:T(4,128)S(1)} collective-permute-done((f32[3,1024]{1,0:T(4,128)S(1)}, f32[3,1024]{1,0:T(4,128)S(1)}, u32[]{:S(2)}, u32[]{:S(2)}) %collective-permute-start.4) | collective-permute-done | bytes 12320 | tf_op jit(solution)/shard_map/ppermute | solution.py:22
  28.4 1.0 %collective-permute-done.5 = f32[5,1024]{1,0:T(8,128)S(1)} collective-permute-done((f32[5,1024]{1,0:T(8,128)S(1)}, f32[5,1024]{1,0:T(8,128)S(1)}, u32[]{:S(2)}, u32[]{:S(2)}) %collective-permute-start.5) | collective-permute-done | bytes 20512 | tf_op jit(solution)/shard_map/ppermute | solution.py:22
  29.4 1.3 %collective-permute-start.6 = (f32[3,512]{1,0:T(4,128)S(1)}, f32[3,512]{1,0:T(4,128)S(1)}, u32[]{:S(2)}, u32[]{:S(2)}) collective-permute-start(f32[3,512]{1,0:T(4,128)S(1)} %constant_dynamic-slice_fusion.1), channel_id=1, source_target_pairs={{0,2},{1,3},{2,0},{3,1},{4,6},{5,7},{6,4},{7,5},{8,10},{9,11},{10,... | collective-permute-start | bytes 18440 | tf_op jit(solution)/shard_map/ppermute | solution.py:27
  30.8 0.8 %collective-permute-start.8 = (f32[2,1024]{1,0:T(2,128)S(1)}, f32[2,1024]{1,0:T(2,128)S(1)}, u32[]{:S(2)}, u32[]{:S(2)}) collective-permute-start(f32[2,1024]{1,0:T(2,128)S(1)} %slice_add_fusion.1), channel_id=1, source_target_pairs={{0,4},{4,0},{8,12},{12,8},{1,5},{5,1},{9,13},{13,9},{2,6},{6,2},{1... | collective-permute-start | bytes 24584 | tf_op jit(solution)/shard_map/ppermute | solution.py:27
  31.6 1.6 %collective-permute-done.6 = f32[3,512]{1,0:T(4,128)S(1)} collective-permute-done((f32[3,512]{1,0:T(4,128)S(1)}, f32[3,512]{1,0:T(4,128)S(1)}, u32[]{:S(2)}, u32[]{:S(2)}) %collective-permute-start.6) | collective-permute-done | bytes 6176 | tf_op jit(solution)/shard_map/ppermute | solution.py:27
  33.2 0.0 collective-permute-start.7
  33.2 1.3 %collective-permute-done.8 = f32[2,1024]{1,0:T(2,128)S(1)} collective-permute-done((f32[2,1024]{1,0:T(2,128)S(1)}, f32[2,1024]{1,0:T(2,128)S(1)}, u32[]{:S(2)}, u32[]{:S(2)}) %collective-permute-start.8) | collective-permute-done | bytes 8224 | tf_op jit(solution)/shard_map/ppermute | solution.py:27
  34.5 0.1 reshape.10
  34.6 0.6 %copy.8 = f32[2,4,8,32]{3,2,1,0:T(8,128)} copy(f32[2,4,8,32]{3,1,2,0:T(4,128)S(1)} %bitcast.5) | data formatting | bytes 16384 | tf_op jit(solution)/shard_map/transpose | solution.py:399
  35.2 0.0 collective-permute-done.7
  35.2 0.6 %dynamic-slice_add_fusion.1 = f32[3,256]{1,0:T(4,128)} fusion(f32[3,256]{1,0:T(4,128)S(1)} %collective-permute-done.7, f32[3,512]{1,0:T(4,128)S(1)} %dynamic-slice_add_fusion, s32[]{:T(128)S(6)} %select_n.33), kind=kLoop, calls=%fused_computation.4 | loop fusion | flops 768 | bytes 9220 | tf_op jit(solution)/shard_map/add | solution.py:397
  (6 shorter events, 0.0 us)
Async XLA Ops:
  0.6 12.1 %collective-permute-start = (bf16[1024,128]{1,0:T(8,128)(2,1)}, bf16[1024,128]{1,0:T(8,128)(2,1)S(1)}, u32[]{:S(2)}, u32[]{:S(2)}) collective-permute-start(bf16[1024,128]{1,0:T(8,128)(2,1)} %bitcast.7), channel_id=1, source_target_pairs={{0,4},{4,8},{8,12},{12,0},{1,5},{5,9},{9,13},{13,1},{2,6},{6,10},{... | collective-permute-start | bytes 786440 | tf_op jit(solution)/shard_map/ppermute | solution.py:22
  3.7 8.9 %collective-permute-start.1 = (bf16[3,1024]{1,0:T(4,128)(2,1)}, bf16[3,1024]{1,0:T(4,128)(2,1)S(1)}, u32[]{:S(2)}, u32[]{:S(2)}) collective-permute-start(bf16[3,1024]{1,0:T(4,128)(2,1)} %refs_2_.1), channel_id=1, source_target_pairs={{0,4},{4,8},{8,12},{12,0},{1,5},{5,9},{9,13},{13,1},{2,6},{6,10},{... | collective-permute-start | bytes 18440 | tf_op jit(solution)/shard_map/ppermute | solution.py:22
  5.3 7.5 %collective-permute-start.2 = (bf16[3,1024]{1,0:T(4,128)(2,1)}, bf16[3,1024]{1,0:T(4,128)(2,1)S(1)}, u32[]{:S(2)}, u32[]{:S(2)}) collective-permute-start(bf16[3,1024]{1,0:T(4,128)(2,1)} %refs_2_.1), channel_id=1, source_target_pairs={{0,8},{4,12},{8,0},{12,4},{1,9},{5,13},{9,1},{13,5},{2,10},{6,14},... | collective-permute-start | bytes 18440 | tf_op jit(solution)/shard_map/ppermute | solution.py:22
  12.8 9.0 %collective-permute-start.3 = (bf16[1024,128]{1,0:T(8,128)(2,1)S(1)}, bf16[1024,128]{1,0:T(8,128)(2,1)S(1)}, u32[]{:S(2)}, u32[]{:S(2)}) collective-permute-start(bf16[1024,128]{1,0:T(8,128)(2,1)S(1)} %collective-permute-done.refs_4_), channel_id=1, source_target_pairs={{0,4},{4,8},{8,12},{12,0},{1,5},{5,9},{9,13},{13,1},{2,6},{6,10},{... | collective-permute-start | bytes 786440 | tf_op jit(solution)/shard_map/ppermute | solution.py:22
  24.5 4.9 %collective-permute-start.5 = (f32[5,1024]{1,0:T(8,128)S(1)}, f32[5,1024]{1,0:T(8,128)S(1)}, u32[]{:S(2)}, u32[]{:S(2)}) collective-permute-start(f32[5,1024]{1,0:T(8,128)S(1)} %get-tuple-element.39), channel_id=1, source_target_pairs={{0,8},{4,12},{8,0},{12,4},{1,9},{5,13},{9,1},{13,5},{2,10},{6,14},... | collective-permute-start | bytes 61448 | tf_op jit(solution)/shard_map/ppermute | solution.py:22
  24.6 3.8 %collective-permute-start.4 = (f32[3,1024]{1,0:T(4,128)S(1)}, f32[3,1024]{1,0:T(4,128)S(1)}, u32[]{:S(2)}, u32[]{:S(2)}) collective-permute-start(f32[3,1024]{1,0:T(4,128)S(1)} %get-tuple-element.38), channel_id=1, source_target_pairs={{0,12},{4,0},{8,4},{12,8},{1,13},{5,1},{9,5},{13,9},{2,14},{6,2},{... | collective-permute-start | bytes 36872 | tf_op jit(solution)/shard_map/ppermute | solution.py:22
  29.4 3.7 %collective-permute-start.6 = (f32[3,512]{1,0:T(4,128)S(1)}, f32[3,512]{1,0:T(4,128)S(1)}, u32[]{:S(2)}, u32[]{:S(2)}) collective-permute-start(f32[3,512]{1,0:T(4,128)S(1)} %constant_dynamic-slice_fusion.1), channel_id=1, source_target_pairs={{0,2},{1,3},{2,0},{3,1},{4,6},{5,7},{6,4},{7,5},{8,10},{9,11},{10,... | collective-permute-start | bytes 18440 | tf_op jit(solution)/shard_map/ppermute | solution.py:27
  30.8 3.7 %collective-permute-start.8 = (f32[2,1024]{1,0:T(2,128)S(1)}, f32[2,1024]{1,0:T(2,128)S(1)}, u32[]{:S(2)}, u32[]{:S(2)}) collective-permute-start(f32[2,1024]{1,0:T(2,128)S(1)} %slice_add_fusion.1), channel_id=1, source_target_pairs={{0,4},{4,0},{8,12},{12,8},{1,5},{5,1},{9,13},{13,9},{2,6},{6,2},{1... | collective-permute-start | bytes 24584 | tf_op jit(solution)/shard_map/ppermute | solution.py:27
  33.2 2.0 %collective-permute-start.7 = (f32[3,256]{1,0:T(4,128)S(1)}, f32[3,256]{1,0:T(4,128)S(1)}, u32[]{:S(2)}, u32[]{:S(2)}) collective-permute-start(f32[3,256]{1,0:T(4,128)S(1)} %constant_dynamic-slice_fusion), channel_id=1, source_target_pairs={{0,1},{1,0},{2,3},{3,2},{4,5},{5,4},{6,7},{7,6},{8,9},{9,8},{10,11... | collective-permute-start | bytes 9224 | tf_op jit(solution)/shard_map/ppermute | solution.py:27

commit v6 on v5

--- a/solution.py
+++ b/solution.py
@@ -388,14 +388,21 @@
     else:
         force_total = lax.psum(force, "blk")
     place = lax.axis_index("freq")
-    flip = freqs // 2
-    while flip:
-        half = total.shape[1] // 2
+    share = row_count // freqs
+    flip = 1
+    while flip < freqs:
         side = (place // flip) % 2
-        kept = lax.dynamic_slice_in_dim(total, side * half, half, axis=1)
-        sent = lax.dynamic_slice_in_dim(total, (1 - side) * half, half, axis=1)
-        total = kept + exchanged(sent, "freq", flip)
-        flip //= 2
+        groups = total.shape[1] // (2 * share)
+
+        def every_other(first):
+            parts = [
+                lax.dynamic_slice_in_dim(total, (2 * k + first) * share, share, axis=1)
+                for k in range(groups)
+            ]
+            return jnp.concatenate(parts, axis=1)
+
+        total = every_other(side) + exchanged(every_other(1 - side), "freq", flip)
+        flip *= 2
     force_total = force_total.reshape(2, 8, columns // 8, columns).transpose(0, 2, 1, 3)
     return (total, force_total.reshape(1, 2, columns, columns))
 

time: 36 us -> 35.2 us (0.978)
  waiting for transfers between devices: 10.9 us -> 9.96 us
    ppermute x3, waiting for transfers between devices: 2.88 us -> 1.97 us  [exchanged(): return lax.ppermute(value, axis, pairs)]
  transfers between devices with their start and end apart: 9 -> 9, of which waited for: 7 -> 8; matrix products, arithmetic and copies ran while one was open for 2% -> 2% of each run, Pallas kernels for 30% -> 30%
where the time goes in v6:
time: 35.2 us; the launch traced here: 35 us
  Pallas kernels  13.4 us (38%)
  waiting for transfers between devices  9.96 us (28%)
  starting transfers between devices  9.52 us (27%)
  local copies, waits for them, and re-layouts  0.74 us (2%)
  between operations  0.7 us (2%)
  other arithmetic  0.63 us (2%)
    pallas_call x3, Pallas kernels, tile_terms(): pl.pallas_call(functools.partial(tile_kernel, offset, plan), out_shape=ou...  13.4 us
    ppermute x6, waiting for transfers between devices, passed_along(): return lax.ppermute(value, axis, pairs)  7.99 us
    ppermute x6, starting transfers between devices, passed_along(): return lax.ppermute(value, axis, pairs)  7.34 us
    ppermute x3, starting transfers between devices, exchanged(): return lax.ppermute(value, axis, pairs)  2.19 us
    ppermute x3, waiting for transfers between devices, exchanged(): return lax.ppermute(value, axis, pairs)  1.97 us
  transfers between devices with their start and end apart: 9, of which 8 were waited for; matrix products, arithmetic and copies ran while one was open for 2% of the time, Pallas kernels for 30%

profile of v6, /device:TPU:0, one launch (start us, length us, event | category | flops | bytes accessed | tf_op | source)
XLA Modules:
  0.0 35.0 jit_solution(2898901121501565774)
XLA Ops:
  0.6 3.1 %collective-permute-start = (bf16[1024,128]{1,0:T(8,128)(2,1)}, bf16[1024,128]{1,0:T(8,128)(2,1)S(1)}, u32[]{:S(2)}, u32[]{:S(2)}) collective-permute-start(bf16[1024,128]{1,0:T(8,128)(2,1)} %bitcast.7), channel_id=1, source_target_pairs={{0,4},{4,8},{8,12},{12,0},{1,5},{5,9},{9,13},{13,1},{2,6},{6,10},{... | collective-permute-start | bytes 786440 | tf_op jit(solution)/shard_map/ppermute | solution.py:22
  3.7 1.6 %collective-permute-start.1 = (bf16[3,1024]{1,0:T(4,128)(2,1)}, bf16[3,1024]{1,0:T(4,128)(2,1)S(1)}, u32[]{:S(2)}, u32[]{:S(2)}) collective-permute-start(bf16[3,1024]{1,0:T(4,128)(2,1)} %refs_2_.1), channel_id=1, source_target_pairs={{0,4},{4,8},{8,12},{12,0},{1,5},{5,9},{9,13},{13,1},{2,6},{6,10},{... | collective-permute-start | bytes 18440 | tf_op jit(solution)/shard_map/ppermute | solution.py:22
  5.3 1.1 %collective-permute-start.2 = (bf16[3,1024]{1,0:T(4,128)(2,1)}, bf16[3,1024]{1,0:T(4,128)(2,1)S(1)}, u32[]{:S(2)}, u32[]{:S(2)}) collective-permute-start(bf16[3,1024]{1,0:T(4,128)(2,1)} %refs_2_.1), channel_id=1, source_target_pairs={{0,8},{4,12},{8,0},{12,4},{1,9},{5,13},{9,1},{13,5},{2,10},{6,14},... | collective-permute-start | bytes 18440 | tf_op jit(solution)/shard_map/ppermute | solution.py:22
  6.4 4.9 %tile_0.1 = (f32[3,1024]{1,0:T(4,128)S(1)}, f32[2,32,32]{2,1,0:T(8,128)S(1)}, f32[8,128]{1,0:T(8,128)S(1)}, bf16[3,1024]{1,0:T(4,128)(2,1)S(1)}, bf16[1024,128]{1,0:T(8,128)(2,1)S(1)}) custom-call(f32[16]{0:T(128)} %refs_0_.1, s32[1,3]{1,0:T(1,128)} %refs_1_.1, bf16[3,1024]{1,0:T(4,128)(2,1)} %refs_2_.1, bf16[1024,128]{1,0:T(8,128)(2,1)} %bitcast.8), custom_call_target="tpu_custom_call" | custom-call | flops 1610612736 | bytes 524288 | tf_op jit(solution)/shard_map/tile_0/pallas_call | solution.py:325
  11.3 1.4 %collective-permute-done.1.refs_3_ = bf16[3,1024]{1,0:T(4,128)(2,1)S(1)} collective-permute-done((bf16[3,1024]{1,0:T(4,128)(2,1)}, bf16[3,1024]{1,0:T(4,128)(2,1)S(1)}, u32[]{:S(2)}, u32[]{:S(2)}) %collective-permute-start.1) | collective-permute-done | bytes 6176 | tf_op jit(solution)/shard_map/ppermute | solution.py:22
  12.6 0.2 collective-permute-done.2.refs_5_.refs_3_
  12.8 0.0 collective-permute-done.refs_4_
  12.8 0.5 %collective-permute-start.3 = (bf16[1024,128]{1,0:T(8,128)(2,1)S(1)}, bf16[1024,128]{1,0:T(8,128)(2,1)S(1)}, u32[]{:S(2)}, u32[]{:S(2)}) collective-permute-start(bf16[1024,128]{1,0:T(8,128)(2,1)S(1)} %collective-permute-done.refs_4_), channel_id=1, source_target_pairs={{0,4},{4,8},{8,12},{12,0},{1,5},{5,9},{9,13},{13,1},{2,6},{6,10},{... | collective-permute-start | bytes 786440 | tf_op jit(solution)/shard_map/ppermute | solution.py:22
  13.3 5.8 %tile_1.1 = (f32[3,1024]{1,0:T(4,128)S(1)}, f32[3,1024]{1,0:T(4,128)S(1)}, f32[2,32,32]{2,1,0:T(8,128)S(1)}, bf16[1024,1024]{1,0:T(8,128)(2,1)S(1)}, f32[1024,10...) custom-call(f32[8,128]{1,0:T(8,128)S(1)} %get-tuple-element.21.refs_0_, ...), custom_call_target="tpu_custom_call" | custom-call | flops 1610612736 | bytes 524288 | tf_op jit(solution)/shard_map/tile_1/pallas_call | solution.py:325
  19.0 2.7 %collective-permute-done.3.refs_4_ = bf16[1024,128]{1,0:T(8,128)(2,1)S(1)} collective-permute-done((bf16[1024,128]{1,0:T(8,128)(2,1)S(1)}, bf16[1024,128]{1,0:T(8,128)(2,1)S(1)}, u32[]{:S(2)}, u32[]{:S(2)}) %collective-permute-start.3) | collective-permute-done | bytes 262176 | tf_op jit(solution)/shard_map/ppermute | solution.py:22
  21.8 2.8 %tile_2.1 = (f32[3,1024]{1,0:T(4,128)S(1)}, f32[5,1024]{1,0:T(8,128)S(1)}) custom-call(f32[8,128]{1,0:T(8,128)S(1)} %get-tuple-element.21.refs_0_, bf16[3,1024]{1,0:T(4,128)(2,1)S(1)} %get-tuple-element.22.refs_1_, bf16[1024,128]{1,0:T(8,128)(2,1)S(1)} %get-tuple-element.23.refs_2_, bf16[3,1024]{1,0:T(4,128)(2,1)S(1)} %collective-permute-done.2.refs_5_.refs_3_, ...), custom_call_target="tpu_custom_call" | custom-call | flops 1610612736 | bytes 524288 | tf_op jit(solution)/shard_map/tile_2/pallas_call | solution.py:325
  24.5 0.1 collective-permute-start.5
  24.6 1.0 %collective-permute-start.4 = (f32[3,1024]{1,0:T(4,128)S(1)}, f32[3,1024]{1,0:T(4,128)S(1)}, u32[]{:S(2)}, u32[]{:S(2)}) collective-permute-start(f32[3,1024]{1,0:T(4,128)S(1)} %get-tuple-element.38), channel_id=1, source_target_pairs={{0,12},{4,0},{8,4},{12,8},{1,13},{5,1},{9,5},{13,9},{2,14},{6,2},{... | collective-permute-start | bytes 36872 | tf_op jit(solution)/shard_map/ppermute | solution.py:22
  25.6 2.7 %collective-permute-done.4 = f32[3,1024]{1,0:T(4,128)S(1)} collective-permute-done((f32[3,1024]{1,0:T(4,128)S(1)}, f32[3,1024]{1,0:T(4,128)S(1)}, u32[]{:S(2)}, u32[]{:S(2)}) %collective-permute-start.4) | collective-permute-done | bytes 12320 | tf_op jit(solution)/shard_map/ppermute | solution.py:22
  28.4 1.0 %collective-permute-done.5 = f32[5,1024]{1,0:T(8,128)S(1)} collective-permute-done((f32[5,1024]{1,0:T(8,128)S(1)}, f32[5,1024]{1,0:T(8,128)S(1)}, u32[]{:S(2)}, u32[]{:S(2)}) %collective-permute-start.5) | collective-permute-done | bytes 20512 | tf_op jit(solution)/shard_map/ppermute | solution.py:22
  29.4 0.1 collective-permute-start.6
  29.5 0.8 %collective-permute-start.8 = (f32[2,1024]{1,0:T(2,128)S(1)}, f32[2,1024]{1,0:T(2,128)S(1)}, u32[]{:S(2)}, u32[]{:S(2)}) collective-permute-start(f32[2,1024]{1,0:T(2,128)S(1)} %slice_add_fusion.1), channel_id=1, source_target_pairs={{0,4},{4,0},{8,12},{12,8},{1,5},{5,1},{9,13},{13,9},{2,6},{6,2},{1... | collective-permute-start | bytes 24584 | tf_op jit(solution)/shard_map/ppermute | solution.py:27
  30.4 0.3 collective-permute-done.6
  30.7 1.3 %collective-permute-start.7 = (f32[3,256]{1,0:T(4,128)S(1)}, f32[3,256]{1,0:T(4,128)S(1)}, u32[]{:S(2)}, u32[]{:S(2)}) collective-permute-start(f32[3,256]{1,0:T(4,128)S(1)} %constant_dynamic-slice_fusion), channel_id=1, source_target_pairs={{0,2},{1,3},{2,0},{3,1},{4,6},{5,7},{6,4},{7,5},{8,10},{9,11},{10,... | collective-permute-start | bytes 9224 | tf_op jit(solution)/shard_map/ppermute | solution.py:27
  32.0 1.3 %collective-permute-done.8 = f32[2,1024]{1,0:T(2,128)S(1)} collective-permute-done((f32[2,1024]{1,0:T(2,128)S(1)}, f32[2,1024]{1,0:T(2,128)S(1)}, u32[]{:S(2)}, u32[]{:S(2)}) %collective-permute-start.8) | collective-permute-done | bytes 8224 | tf_op jit(solution)/shard_map/ppermute | solution.py:27
  33.3 0.1 reshape.10
  33.4 0.6 %copy.8 = f32[2,4,8,32]{3,2,1,0:T(8,128)} copy(f32[2,4,8,32]{3,1,2,0:T(4,128)S(1)} %bitcast.5) | data formatting | bytes 16384 | tf_op jit(solution)/shard_map/transpose | solution.py:406
  34.0 0.4 %collective-permute-done.7 = f32[3,256]{1,0:T(4,128)S(1)} collective-permute-done((f32[3,256]{1,0:T(4,128)S(1)}, f32[3,256]{1,0:T(4,128)S(1)}, u32[]{:S(2)}, u32[]{:S(2)}) %collective-permute-start.7) | collective-permute-done | bytes 3104 | tf_op jit(solution)/shard_map/ppermute | solution.py:27
  34.4 0.6 %dynamic-slice_add_fusion = f32[3,256]{1,0:T(4,128)} fusion(f32[3,256]{1,0:T(4,128)S(1)} %collective-permute-done.7, f32[3,512]{1,0:T(4,128)S(1)} %maximum_add_fusion, s32[]{:T(128)S(6)} %select_n.41), kind=kLoop, calls=%fused_computation.5 | loop fusion | flops 768 | bytes 9220 | tf_op jit(solution)/shard_map/add | solution.py:404
  (7 shorter events, 0.1 us)
Async XLA Ops:
  0.6 12.1 %collective-permute-start = (bf16[1024,128]{1,0:T(8,128)(2,1)}, bf16[1024,128]{1,0:T(8,128)(2,1)S(1)}, u32[]{:S(2)}, u32[]{:S(2)}) collective-permute-start(bf16[1024,128]{1,0:T(8,128)(2,1)} %bitcast.7), channel_id=1, source_target_pairs={{0,4},{4,8},{8,12},{12,0},{1,5},{5,9},{9,13},{13,1},{2,6},{6,10},{... | collective-permute-start | bytes 786440 | tf_op jit(solution)/shard_map/ppermute | solution.py:22
  3.7 8.9 %collective-permute-start.1 = (bf16[3,1024]{1,0:T(4,128)(2,1)}, bf16[3,1024]{1,0:T(4,128)(2,1)S(1)}, u32[]{:S(2)}, u32[]{:S(2)}) collective-permute-start(bf16[3,1024]{1,0:T(4,128)(2,1)} %refs_2_.1), channel_id=1, source_target_pairs={{0,4},{4,8},{8,12},{12,0},{1,5},{5,9},{9,13},{13,1},{2,6},{6,10},{... | collective-permute-start | bytes 18440 | tf_op jit(solution)/shard_map/ppermute | solution.py:22
  5.3 7.5 %collective-permute-start.2 = (bf16[3,1024]{1,0:T(4,128)(2,1)}, bf16[3,1024]{1,0:T(4,128)(2,1)S(1)}, u32[]{:S(2)}, u32[]{:S(2)}) collective-permute-start(bf16[3,1024]{1,0:T(4,128)(2,1)} %refs_2_.1), channel_id=1, source_target_pairs={{0,8},{4,12},{8,0},{12,4},{1,9},{5,13},{9,1},{13,5},{2,10},{6,14},... | collective-permute-start | bytes 18440 | tf_op jit(solution)/shard_map/ppermute | solution.py:22
  12.8 9.0 %collective-permute-start.3 = (bf16[1024,128]{1,0:T(8,128)(2,1)S(1)}, bf16[1024,128]{1,0:T(8,128)(2,1)S(1)}, u32[]{:S(2)}, u32[]{:S(2)}) collective-permute-start(bf16[1024,128]{1,0:T(8,128)(2,1)S(1)} %collective-permute-done.refs_4_), channel_id=1, source_target_pairs={{0,4},{4,8},{8,12},{12,0},{1,5},{5,9},{9,13},{13,1},{2,6},{6,10},{... | collective-permute-start | bytes 786440 | tf_op jit(solution)/shard_map/ppermute | solution.py:22
  24.5 4.9 %collective-permute-start.5 = (f32[5,1024]{1,0:T(8,128)S(1)}, f32[5,1024]{1,0:T(8,128)S(1)}, u32[]{:S(2)}, u32[]{:S(2)}) collective-permute-start(f32[5,1024]{1,0:T(8,128)S(1)} %get-tuple-element.39), channel_id=1, source_target_pairs={{0,8},{4,12},{8,0},{12,4},{1,9},{5,13},{9,1},{13,5},{2,10},{6,14},... | collective-permute-start | bytes 61448 | tf_op jit(solution)/shard_map/ppermute | solution.py:22
  24.6 3.8 %collective-permute-start.4 = (f32[3,1024]{1,0:T(4,128)S(1)}, f32[3,1024]{1,0:T(4,128)S(1)}, u32[]{:S(2)}, u32[]{:S(2)}) collective-permute-start(f32[3,1024]{1,0:T(4,128)S(1)} %get-tuple-element.38), channel_id=1, source_target_pairs={{0,12},{4,0},{8,4},{12,8},{1,13},{5,1},{9,5},{13,9},{2,14},{6,2},{... | collective-permute-start | bytes 36872 | tf_op jit(solution)/shard_map/ppermute | solution.py:22
  29.4 1.2 %collective-permute-start.6 = (f32[3,512]{1,0:T(4,128)S(1)}, f32[3,512]{1,0:T(4,128)S(1)}, u32[]{:S(2)}, u32[]{:S(2)}) collective-permute-start(f32[3,512]{1,0:T(4,128)S(1)} %pad_maximum_fusion), channel_id=1, source_target_pairs={{0,1},{1,0},{2,3},{3,2},{4,5},{5,4},{6,7},{7,6},{8,9},{9,8},{10,11... | collective-permute-start | bytes 18440 | tf_op jit(solution)/shard_map/ppermute | solution.py:27
  29.5 3.7 %collective-permute-start.8 = (f32[2,1024]{1,0:T(2,128)S(1)}, f32[2,1024]{1,0:T(2,128)S(1)}, u32[]{:S(2)}, u32[]{:S(2)}) collective-permute-start(f32[2,1024]{1,0:T(2,128)S(1)} %slice_add_fusion.1), channel_id=1, source_target_pairs={{0,4},{4,0},{8,12},{12,8},{1,5},{5,1},{9,13},{13,9},{2,6},{6,2},{1... | collective-permute-start | bytes 24584 | tf_op jit(solution)/shard_map/ppermute | solution.py:27
  30.7 3.7 %collective-permute-start.7 = (f32[3,256]{1,0:T(4,128)S(1)}, f32[3,256]{1,0:T(4,128)S(1)}, u32[]{:S(2)}, u32[]{:S(2)}) collective-permute-start(f32[3,256]{1,0:T(4,128)S(1)} %constant_dynamic-slice_fusion), channel_id=1, source_target_pairs={{0,2},{1,3},{2,0},{3,1},{4,6},{5,7},{6,4},{7,5},{8,10},{9,11},{10,... | collective-permute-start | bytes 9224 | tf_op jit(solution)/shard_map/ppermute | solution.py:27
